TPU v7x, 128 devices: a whole 4x4x4 slice. The times are simulated.
128 devices in a mesh: group: 2 (over y_hi), tile: 64 (over z, y_lo, x, core).
Axes of the slice: x: 4, y: 4 (y_hi: 2, y_lo: 2; y = y_hi * 2 + y_lo), z: 4, core: 2. Of those that a mesh axis runs over, the one named last changes fastest.
Arguments:
- vorticity: float32 [16, 1024, 1024], P(None, ('group', 'tile')), may hold values from -6 to 6
- layer_to_mode: float32 [16, 16], replicated, may hold values from -1.5 to 1.5
- mode_to_layer: float32 [16, 16], replicated, may hold values from -1.5 to 1.5
- inverse_radii: float32 [16], replicated, may hold values from 0.001 to 1
- wind_curl: float32 [1024, 1024], P(('group', 'tile')), may hold values from -6 to 6
- wet_mask: int32 [1024, 1024], P(('group', 'tile')), may hold values 0 or 1
Outputs:
- new_vorticity: float32 [16, 1024, 1024], P(None, ('group', 'tile'))
- stream: float32 [16, 1024, 1024], P(None, ('group', 'tile'))
All inputs are finite; a program needn't handle non-finite values. No bound on the sum of `wet_mask` on one device may be relied on, other than what follows from the above.
Results may differ from a plain program's by a relative error of at most 0.00011.
Values sent between devices are 32-bit elements; how exact they have to be, the bound alone decides.
No kernel may reach another device: no remote copies, remote signals or barrier semaphores. Data moves between devices by JAX's collectives and lax.ppermute only.
A program may use at most 64 MiB of HBM per device.

v0:
```python
import functools
import math

import jax
import jax.numpy as jnp
import numpy as np
from jax import lax
from jax.experimental import pallas as pl
from jax.experimental.pallas import tpu as pltpu
from jax.sharding import PartitionSpec as P

time_step = 0.5
beta_plane = 1.0
bottom_drag = 0.2

N = 1024
NL = 16
ROWS = 8
BLOCKS = 128
LANES = 128
AXES = ("group", "tile")
HIGHEST = lax.Precision.HIGHEST
VMEM = pl.BlockSpec(memory_space=pltpu.VMEM)
SMEM = pl.BlockSpec(memory_space=pltpu.SMEM)


def host_tables():
    k = np.arange(1, N + 1)
    a = 32 * np.arange(32)
    b = np.arange(1, 33)
    turn = 2 * (N + 1)
    angle_a = np.pi * ((a[:, None] * k[None, :]) % turn) / (N + 1)
    angle_b = np.pi * ((b[:, None] * k[None, :]) % turn) / (N + 1)
    scale = math.sqrt(2.0 / (N + 1))
    eigen = 4.0 * np.sin(np.pi * k / (2 * (N + 1))) ** 2
    return [
        np.asarray(t, np.float32)
        for t in (
            np.sin(angle_a),
            np.cos(angle_a),
            scale * np.sin(angle_b),
            scale * np.cos(angle_b),
            eigen,
        )
    ]


def iota(shape, dim):
    return lax.broadcasted_iota(jnp.int32, shape, dim)


def dot(left, right, precision=None):
    return lax.dot_general(
        left,
        right,
        (((1,), (0,)), ((), ())),
        precision=precision,
        preferred_element_type=jnp.float32,
    )


def halves(value):
    high = value.astype(jnp.bfloat16)
    low = (value - high.astype(jnp.float32)).astype(jnp.bfloat16)
    return high, low


def radii_column(radii_ref, shape):
    sub = iota(shape, 0)
    column = jnp.zeros(shape, jnp.float32)
    for m in range(NL):
        column = jnp.where(sub == m, radii_ref[m], column)
    return column


def decay_of(shift):
    half = 0.5 * jnp.sqrt(shift)
    root = jnp.sqrt(1.0 + 0.25 * shift)
    grow = half + root
    return 1.0 / (grow * grow), 1.0 / (4.0 * half * root)


def transform(rows, table_high, table_low):
    high, low = rows
    count = high.shape[0]
    both = dot(jnp.concatenate([high, low], 0), table_high)
    return both[:count] + both[count:] + dot(high, table_low)


def forward_kernel(
    vortex_ref, mix_ref, radii_ref, eigen_ref, sa_ref, ca_ref, sb_ref, cb_ref,
    send_ref, force_ref, high_ref, low_ref,
):
    rows = NL * ROWS
    spread = (iota((NL, rows), 1) // ROWS == iota((NL, rows), 0)).astype(jnp.float32)
    wide = dot(mix_ref[...], spread, HIGHEST)
    mix = jnp.concatenate([wide] * ROWS, 0)
    mix = jnp.where(iota((rows, rows), 0) // NL == iota((rows, rows), 1) % ROWS, mix, 0.0)
    modal = dot(mix, vortex_ref[...].reshape(rows, N), HIGHEST)
    split = halves(modal)
    rho, weight = decay_of(eigen_ref[...].reshape(1, N) + radii_column(radii_ref, (NL, N)))
    step = 256
    for n in range(N // step):
        cols = slice(n * step, (n + 1) * step)
        for a in range(32):
            block = sa_ref[a : a + 1, cols] * cb_ref[:, cols] + ca_ref[a : a + 1, cols] * sb_ref[:, cols]
            high, low = halves(block)
            high_ref[32 * a : 32 * a + 32, cols] = high
            low_ref[32 * a : 32 * a + 32, cols] = low
        spectrum = transform(split, high_ref[:, cols], low_ref[:, cols])
        right = jnp.zeros((NL, step), jnp.float32)
        left = jnp.zeros((NL, step), jnp.float32)
        force = []
        for y in range(ROWS):
            force.append(-weight[:, cols] * spectrum[y * NL : (y + 1) * NL])
            force_ref[y, :, cols] = force[y]
            right = rho[:, cols] * right + force[y]
        for y in reversed(range(ROWS)):
            left = rho[:, cols] * left + force[y]
        for c in range(step // LANES):
            dest = n * (step // LANES) + c
            part = slice(c * LANES, (c + 1) * LANES)
            send_ref[dest * NL : (dest + 1) * NL, 0, :LANES] = right[:, part]
            send_ref[dest * NL : (dest + 1) * NL, 0, LANES:] = left[:, part]


def shift_rows(value, step):
    blank = jnp.zeros((abs(step), value.shape[1]), value.dtype)
    if step > 0:
        return jnp.concatenate([blank, value[:-step]], 0)
    return jnp.concatenate([value[-step:], blank], 0)


def scan_kernel(index_ref, radii_ref, eigen_ref, take_ref, give_ref):
    me = index_ref[0]
    mode = me % NL
    chunk = me // NL
    shift = eigen_ref[pl.ds(chunk, 1), :] + radii_ref[mode]
    rho, _ = decay_of(shift)
    rho2 = rho * rho
    rho4 = rho2 * rho2
    block = rho4 * rho4
    right = take_ref[:, 0, :LANES]
    left = take_ref[:, 0, LANES:]
    place = iota((BLOCKS, LANES), 0)
    power = jnp.ones((BLOCKS, LANES), jnp.float32)
    rate = block
    step = 1
    while step < BLOCKS:
        right = right + rate * shift_rows(right, step)
        left = left + rate * shift_rows(left, -step)
        power = jnp.where((place // step) % 2 == 1, power * rate, power)
        rate = rate * rate
        step *= 2
    below = rho * left[:1]
    above = rho * right[BLOCKS - 1 :]
    far = rate * rho
    scale = 1.0 / (1.0 - far * far)
    alpha = -(below - far * above) * scale
    beta = -(above - far * below) * scale
    back = jnp.where(place == BLOCKS - 1, 1.0, 0.0)
    reverse = jnp.ones((BLOCKS, LANES), jnp.float32)
    rate = block
    step = 1
    while step < BLOCKS:
        reverse = jnp.where(((BLOCKS - 1 - place) // step) % 2 == 1, reverse * rate, reverse)
        rate = rate * rate
        step *= 2
    give_ref[:, 0, :LANES] = shift_rows(right, 1) + alpha * power
    give_ref[:, 0, LANES:] = shift_rows(left, -1) + beta * reverse


def roll_lanes(value, step):
    width = value.shape[1]
    lane = iota(value.shape, 1)
    rolled = pltpu.roll(value, step % width, 1)
    return jnp.where(lane == (0 if step > 0 else width - 1), 0.0, rolled)


def roll_sub(value, edge, step):
    height = value.shape[0]
    sub = iota(value.shape, 0)
    rolled = pltpu.roll(value, step % height, 0)
    return jnp.where(sub == (0 if step > 0 else height - 1), edge, rolled)


def local_kernel(
    force_ref, vortex_ref, south_ref, north_ref, wind_ref, wet_ref, radii_ref, eigen_ref, mix_ref,
    part_ref, mixed_ref, base_ref, coef_ref, drag_ref,
):
    rho, _ = decay_of(eigen_ref[...].reshape(1, N) + radii_column(radii_ref, (NL, N)))
    right = jnp.zeros((NL, N), jnp.float32)
    for y in range(ROWS):
        right = rho * right + force_ref[y]
        part_ref[y + 1] = right
    part_ref[ROWS + 1] = rho * right
    left = jnp.zeros((NL, N), jnp.float32)
    for y in reversed(range(ROWS)):
        part_ref[y + 1] += left
        left = rho * (left + force_ref[y])
    part_ref[0] = left
    tall = NL * (ROWS + 2)
    row = iota((tall, NL), 0)
    layer = jnp.where(row < NL * ROWS, row // ROWS, row % NL)
    pick = (layer == iota((tall, NL), 1)).astype(jnp.float32)
    wide = (iota((NL, tall), 1) % NL == iota((NL, tall), 0)).astype(jnp.float32)
    mixed = dot(dot(pick, mix_ref[...], HIGHEST), wide, HIGHEST)
    row = iota((tall, tall), 0)
    place = jnp.where(row < NL * ROWS, row % ROWS + 1, jnp.where(row < NL * (ROWS + 1), 0, ROWS + 1))
    mixed_ref[...] = jnp.where(iota((tall, tall), 1) // NL == place, mixed, 0.0)
    keep = time_step * wet_ref[...].astype(jnp.float32)
    twelfth = keep * (1.0 / 12.0)
    for layer in range(NL):
        mid = vortex_ref[layer]
        north = roll_sub(mid, north_ref[layer : layer + 1], -1)
        south = roll_sub(mid, south_ref[layer : layer + 1], 1)
        east = roll_lanes(mid, -1)
        west = roll_lanes(mid, 1)
        north_east = roll_lanes(north, -1)
        north_west = roll_lanes(north, 1)
        south_east = roll_lanes(south, -1)
        south_west = roll_lanes(south, 1)
        along = north - south
        across = east - west
        c_east = -twelfth * (along + (north_east - south_east)) - keep * (0.5 * beta_plane)
        c_west = twelfth * (along + (north_west - south_west)) + keep * (0.5 * beta_plane)
        c_north = twelfth * (across + (north_east - north_west))
        c_south = -twelfth * (across + (south_east - south_west))
        if layer == NL - 1:
            drag = keep * bottom_drag
            c_east = c_east - drag
            c_west = c_west - drag
            c_north = c_north - drag
            c_south = c_south - drag
            drag_ref[...] = 4.0 * drag
        coef_ref[0, layer] = c_north
        coef_ref[1, layer] = c_south
        coef_ref[2, layer] = roll_lanes(c_east, 1)
        coef_ref[3, layer] = roll_lanes(-twelfth * (north - east), 1)
        coef_ref[4, layer] = roll_lanes(twelfth * (south - east), 1)
        coef_ref[5, layer] = roll_lanes(c_west, -1)
        coef_ref[6, layer] = roll_lanes(twelfth * (north - west), -1)
        coef_ref[7, layer] = roll_lanes(-twelfth * (south - west), -1)
        base_ref[layer] = mid + keep * wind_ref[...] if layer == 0 else mid


def backward_kernel(
    index_ref, take_ref, part_ref, radii_ref, eigen_ref, high_ref, low_ref, mixed_ref, base_ref, coef_ref, drag_ref,
    vortex_ref, stream_ref, psi_ref, wave_ref,
):
    tall = NL * (ROWS + 2)
    rho, _ = decay_of(eigen_ref[...].reshape(1, N) + radii_column(radii_ref, (NL, N)))
    for c in range(N // LANES):
        cols = slice(c * LANES, (c + 1) * LANES)
        up = take_ref[c * NL : (c + 1) * NL, 0, :LANES]
        down = take_ref[c * NL : (c + 1) * NL, 0, LANES:]
        near = rho[:, cols]
        ups, downs = [up], [down]
        for _ in range(ROWS + 1):
            ups.append(ups[-1] * near)
            downs.append(downs[-1] * near)
        for i in range(ROWS + 2):
            psi_ref[i * NL : (i + 1) * NL, cols] = part_ref[i, :, cols] + ups[i] + downs[ROWS + 1 - i]
    split = halves(dot(mixed_ref[...], psi_ref[...], HIGHEST))
    step = 256
    for n in range(N // step):
        cols = slice(n * step, (n + 1) * step)
        wave_ref[:, cols] = transform(split, high_ref[:, cols], low_ref[:, cols])
    inside_low = jnp.where(index_ref[0] > 0, 1.0, 0.0)
    inside_high = jnp.where(index_ref[0] < BLOCKS - 1, 1.0, 0.0)
    body = NL * ROWS
    for layer in range(NL):
        mid = wave_ref[layer * ROWS : (layer + 1) * ROWS]
        north = roll_sub(mid, inside_high * wave_ref[body + NL + layer : body + NL + layer + 1], -1)
        south = roll_sub(mid, inside_low * wave_ref[body + layer : body + layer + 1], 1)
        stream_ref[layer] = mid
        total = base_ref[layer] + coef_ref[0, layer] * north + coef_ref[1, layer] * south
        if layer == NL - 1:
            total = total + drag_ref[...] * mid
        from_east = coef_ref[2, layer] * mid + coef_ref[3, layer] * north + coef_ref[4, layer] * south
        from_west = coef_ref[5, layer] * mid + coef_ref[6, layer] * north + coef_ref[7, layer] * south
        total = total + pltpu.roll(from_east, N - 1, 1) + pltpu.roll(from_west, 1, 1)
        vortex_ref[layer] = total


def call(kernel, outs, specs, args, flops, nbytes, scratch=(), limit=24 << 20):
    return pl.pallas_call(
        kernel,
        out_shape=[jax.ShapeDtypeStruct(s, d) for s, d in outs],
        in_specs=specs,
        out_specs=[VMEM] * len(outs),
        scratch_shapes=list(scratch),
        compiler_params=pltpu.CompilerParams(vmem_limit_bytes=limit),
        cost_estimate=pl.CostEstimate(flops=flops, bytes_accessed=nbytes, transcendentals=0),
    )(*args)


def body(vorticity, layer_to_mode, mode_to_layer, inverse_radii, wind_curl, wet_mask):
    f32, bf16 = jnp.float32, jnp.bfloat16
    sin_a, cos_a, sin_b, cos_b, eigen = (jnp.asarray(t) for t in host_tables())
    eigen = eigen.reshape(N // LANES, LANES)
    index = (lax.axis_index("group") * lax.axis_size("tile") + lax.axis_index("tile")).astype(jnp.int32).reshape(1)
    south = lax.ppermute(vorticity[:, ROWS - 1], AXES, [(i, i + 1) for i in range(BLOCKS - 1)])
    north = lax.ppermute(vorticity[:, 0], AXES, [(i + 1, i) for i in range(BLOCKS - 1)])
    eigen_row = eigen.reshape(1, N)
    send, force, high, low = call(
        forward_kernel,
        [((BLOCKS, 1, 2 * LANES), f32), ((ROWS, NL, N), f32), ((N, N), bf16), ((N, N), bf16)],
        [VMEM, VMEM, SMEM] + [VMEM] * 5,
        (vorticity, layer_to_mode, inverse_radii, eigen_row, sin_a, cos_a, sin_b, cos_b),
        6 * 2 * 128 * N * N, 8 << 20,
    )
    take = lax.all_to_all(send, AXES, split_axis=0, concat_axis=0, tiled=True)
    part, mixed, base, coef, drag = call(
        local_kernel,
        [((ROWS + 2, NL, N), f32), ((160, 160), f32), ((NL, ROWS, N), f32), ((8, NL, ROWS, N), f32), ((ROWS, N), f32)],
        [VMEM] * 6 + [SMEM] + [VMEM] * 2,
        (force, vorticity, south, north, wind_curl, wet_mask, inverse_radii, eigen_row, mode_to_layer),
        1 << 27, 8 << 20,
    )
    (give,) = call(
        scan_kernel,
        [((BLOCKS, 1, 2 * LANES), f32)],
        [SMEM, SMEM, VMEM, VMEM],
        (index, inverse_radii, eigen, take),
        1 << 20, 1 << 18,
    )
    amplitude = lax.all_to_all(give, AXES, split_axis=0, concat_axis=0, tiled=True)
    new_vorticity, stream = call(
        backward_kernel,
        [((NL, ROWS, N), f32), ((NL, ROWS, N), f32)],
        [SMEM, VMEM, VMEM, SMEM] + [VMEM] * 7,
        (index, amplitude, part, inverse_radii, eigen_row, high, low, mixed, base, coef, drag),
        6 * 2 * 160 * N * N, 10 << 20,
        scratch=(pltpu.VMEM((160, N), f32), pltpu.VMEM((160, N), f32)),
    )
    return new_vorticity, stream


def solution(mesh):
    rows = P(None, AXES, None)
    return jax.shard_map(
        body,
        mesh=mesh,
        in_specs=(rows, P(), P(), P(), P(AXES, None), P(AXES, None)),
        out_specs=(rows, rows),
        check_vma=False,
    )
```

profile of v0, /device:TPU:31, one launch (start us, length us, event | category | flops | bytes accessed | tf_op | source)
XLA Modules:
  0.0 69.2 jit_solution(12216647148877786652)
XLA Ops:
  0.6 0.0 copy-start.15
  0.6 0.0 copy-start.4
  0.7 1.0 %copy-done.4 = f32[16,8,1024]{2,1,0:T(8,128)S(1)} copy-done((f32[16,8,1024]{2,1,0:T(8,128)S(1)}, f32[16,8,1024]{2,1,0:T(8,128)}, u32[]{:S(2)}) %copy-start.4) | copy-done | bytes 524312
  1.7 0.0 copy-start.14
  1.7 0.7 copy-done.14
  2.4 0.7 copy-done.17
  3.0 0.0 copy-start.20
  3.0 0.7 %copy-done.20 = f32[16,16]{1,0:T(8,128)S(1)} copy-done((f32[16,16]{1,0:T(8,128)S(1)}, f32[16,16]{1,0:T(8,128)}, u32[]{:S(2)}) %copy-start.20) | copy-done | bytes 1048
  3.7 0.0 copy-start.21
  3.7 0.9 %copy-done.21 = f32[32,1024]{1,0:T(8,128)S(1)} copy-done((f32[32,1024]{1,0:T(8,128)S(1)}, f32[32,1024]{1,0:T(8,128)}, u32[]{:S(2)}) %copy-start.21) | copy-done | bytes 131096
  4.6 0.0 copy-start.22
  4.6 0.9 %copy-done.22 = f32[32,1024]{1,0:T(8,128)S(1)} copy-done((f32[32,1024]{1,0:T(8,128)S(1)}, f32[32,1024]{1,0:T(8,128)}, u32[]{:S(2)}) %copy-start.22) | copy-done | bytes 131096
  5.5 0.9 %copy-done.23 = f32[32,1024]{1,0:T(8,128)S(1)} copy-done((f32[32,1024]{1,0:T(8,128)S(1)}, f32[32,1024]{1,0:T(8,128)}, u32[]{:S(2)}) %copy-start.23) | copy-done | bytes 131096
  6.4 0.9 %copy-done.24 = f32[32,1024]{1,0:T(8,128)S(1)} copy-done((f32[32,1024]{1,0:T(8,128)S(1)}, f32[32,1024]{1,0:T(8,128)}, u32[]{:S(2)}) %copy-start.24) | copy-done | bytes 131096
  7.4 0.0 copy-start.13
  7.4 0.0 copy-start.16
  7.4 3.3 %shard_map.122 = (f32[128,1,256]{2,1,0:T(1,128)}, f32[8,16,1024]{2,1,0:T(8,128)S(1)}, bf16[1024,1024]{1,0:T(8,128)(2,1)S(1)}, bf16[1024,1024]{1,0:T(8,128)(2,1)S(1)}) custom-call(f32[16,8,1024]{2,1,0:T(8,128)S(1)} %copy-done.4, f32[16,16]{1,0:T(8,128)S(1)} %copy-done.20, f32[16]{0:T(128)S(1)} %copy-done.17, f32[1,1024]{1,0:T(1,128)S(1)} %copy-done.14, ...), custom_call_target="tpu_custom_call" | custom-call | flops 1610612736 | bytes 8388608 | tf_op jit(solution)/shard_map/pallas_call | solution.py:287
  10.7 1.4 %copy-done.2 = bf16[1024,1024]{1,0:T(8,128)(2,1)} copy-done((bf16[1024,1024]{1,0:T(8,128)(2,1)}, bf16[1024,1024]{1,0:T(8,128)(2,1)S(1)}, u32[]{:S(2)}) %copy-start.2) | copy-done | bytes 2097176
  12.1 0.8 %copy-done.8 = f32[8,16,1024]{2,1,0:T(8,128)} copy-done((f32[8,16,1024]{2,1,0:T(8,128)}, f32[8,16,1024]{2,1,0:T(8,128)S(1)}, u32[]{:S(2)}) %copy-start.8) | copy-done | bytes 524312
  12.9 10.5 %all-to-all-start = ((f32[128,1,256]{2,1,0:T(1,128)}), f32[128,1,256]{2,1,0:T(1,128)S(1)}, u32[]{:S(2)}, u32[]{:S(2)}) async-start(f32[128,1,256]{2,1,0:T(1,128)} %get-tuple-element.11), calls=%async_computation | async-start | bytes 262144 | tf_op jit(solution)/shard_map/all_to_all | solution.py:313
  23.4 6.6 %all-to-all-done.take_ref = f32[128,1,256]{2,1,0:T(1,128)S(1)} async-done(((f32[128,1,256]{2,1,0:T(1,128)}), f32[128,1,256]{2,1,0:T(1,128)S(1)}, u32[]{:S(2)}, u32[]{:S(2)}) %all-to-all-start) | async-done | bytes 131104 | tf_op jit(solution)/shard_map/all_to_all | solution.py:313
  30.0 0.0 copy-done.18
  30.0 0.0 copy-done.19
  30.0 1.7 %shard_map.123 = f32[128,1,256]{2,1,0:T(1,128)} custom-call(s32[1]{0:T(128)} %bitcast.index_ref, f32[16]{0:T(128)S(1)} %copy-done.18, f32[8,128]{1,0:T(8,128)S(1)} %copy-done.19, f32[128,1,256]{2,1,0:T(1,128)S(1)} %all-to-all-done.take_ref), custom_call_target="tpu_custom_call" | custom-call | flops 1048576 | bytes 262144 | tf_op jit(solution)/shard_map/pallas_call | solution.py:287
  31.7 7.6 %all-to-all-start.1 = ((f32[128,1,256]{2,1,0:T(1,128)}), f32[128,1,256]{2,1,0:T(1,128)S(1)}, u32[]{:S(2)}, u32[]{:S(2)}) async-start(f32[128,1,256]{2,1,0:T(1,128)} %shard_map.123), calls=%async_computation.1 | async-start | bytes 262144 | tf_op jit(solution)/shard_map/all_to_all | solution.py:328
  39.3 0.0 copy-done.5
  39.3 0.1 fusion
  39.4 3.8 %collective-permute-start = (f32[16,1024]{1,0:T(8,128)S(1)}, f32[16,1024]{1,0:T(8,128)S(1)}, u32[]{:S(2)}, u32[]{:S(2)}) collective-permute-start(f32[16,1024]{1,0:T(8,128)S(1)} %bitcast.7), channel_id=1, source_target_pairs={{0,1},{1,2},{2,3},{3,4},{4,5},{5,6},{6,7},{7,8},{8,9},{9,10},{10,1... | collective-permute-start | bytes 196616 | tf_op jit(solution)/shard_map/ppermute | solution.py:303
  43.2 1.9 %collective-permute-start.1 = (f32[16,1024]{1,0:T(8,128)S(1)}, f32[16,1024]{1,0:T(8,128)S(1)}, u32[]{:S(2)}, u32[]{:S(2)}) collective-permute-start(f32[16,1024]{1,0:T(8,128)S(1)} %bitcast.8), channel_id=1, source_target_pairs={{1,0},{2,1},{3,2},{4,3},{5,4},{6,5},{7,6},{8,7},{9,8},{10,9},{11,1... | collective-permute-start | bytes 196616 | tf_op jit(solution)/shard_map/ppermute | solution.py:304
  45.2 0.0 collective-permute-done.south_ref
  45.2 6.7 %collective-permute-done.1.north_ref = f32[16,1024]{1,0:T(8,128)S(1)} collective-permute-done((f32[16,1024]{1,0:T(8,128)S(1)}, f32[16,1024]{1,0:T(8,128)S(1)}, u32[]{:S(2)}, u32[]{:S(2)}) %collective-permute-start.1) | collective-permute-done | bytes 65568 | tf_op jit(solution)/shard_map/ppermute | solution.py:304
  51.8 0.0 copy-done.15
  51.8 0.0 copy-done.12
  51.8 0.0 copy-done.13
  51.8 0.0 copy-done.16
  51.9 0.0 copy-start.9
  51.9 1.0 %copy-done.9 = f32[8,16,1024]{2,1,0:T(8,128)S(1)} copy-done((f32[8,16,1024]{2,1,0:T(8,128)S(1)}, f32[8,16,1024]{2,1,0:T(8,128)}, u32[]{:S(2)}) %copy-start.9) | copy-done | bytes 524312
  52.9 3.3 %shard_map.124 = (f32[10,16,1024]{2,1,0:T(8,128)S(1)}, f32[160,160]{1,0:T(8,128)S(1)}, f32[16,8,1024]{2,1,0:T(8,128)S(1)}, f32[8,16,8,1024]{3,2,1,0:T(8,128)S(1)}, f32[8,1024]{1,0:T(8,128)S(1)}) custom-call(f32[8,16,1024]{2,1,0:T(8,128)S(1)} %copy-done.9, f32[16,8,1024]{2,1,0:T(8,128)S(1)} %copy-done.5, f32[16,1024]{1,0:T(8,128)S(1)} %collective-permute-done.south_ref, ...), custom_call_target="tpu_custom_call" | custom-call | flops 134217728 | bytes 8388608 | tf_op jit(solution)/shard_map/pallas_call | solution.py:287
  56.2 0.0 copy-start
  56.2 1.9 %copy-done = f32[8,16,8,1024]{3,2,1,0:T(8,128)} copy-done((f32[8,16,8,1024]{3,2,1,0:T(8,128)}, f32[8,16,8,1024]{3,2,1,0:T(8,128)S(1)}, u32[]{:S(2)}) %copy-start) | copy-done | bytes 4194328
  58.1 0.8 %copy-done.6 = f32[16,8,1024]{2,1,0:T(8,128)} copy-done((f32[16,8,1024]{2,1,0:T(8,128)}, f32[16,8,1024]{2,1,0:T(8,128)S(1)}, u32[]{:S(2)}) %copy-start.6) | copy-done | bytes 524312
  58.9 0.7 copy-done.10
  59.6 0.0 all-to-all-done.1.take_ref
  59.6 2.2 %copy-done.1 = f32[8,16,8,1024]{3,2,1,0:T(8,128)S(1)} copy-done((f32[8,16,8,1024]{3,2,1,0:T(8,128)S(1)}, f32[8,16,8,1024]{3,2,1,0:T(8,128)}, u32[]{:S(2)}) %copy-start.1) | copy-done | bytes 4194328
  61.8 1.6 %copy-done.3 = bf16[1024,1024]{1,0:T(8,128)(2,1)S(1)} copy-done((bf16[1024,1024]{1,0:T(8,128)(2,1)S(1)}, bf16[1024,1024]{1,0:T(8,128)(2,1)}, u32[]{:S(2)}) %copy-start.3) | copy-done | bytes 2097176
  63.4 1.0 %copy-done.7 = f32[16,8,1024]{2,1,0:T(8,128)S(1)} copy-done((f32[16,8,1024]{2,1,0:T(8,128)S(1)}, f32[16,8,1024]{2,1,0:T(8,128)}, u32[]{:S(2)}) %copy-start.7) | copy-done | bytes 524312
  64.4 0.9 %copy-done.11 = f32[160,160]{1,0:T(8,128)S(1)} copy-done((f32[160,160]{1,0:T(8,128)S(1)}, f32[160,160]{1,0:T(8,128)}, u32[]{:S(2)}) %copy-start.11) | copy-done | bytes 102424
  65.3 3.9 %shard_map.125 = (f32[16,8,1024]{2,1,0:T(8,128)}, f32[16,8,1024]{2,1,0:T(8,128)}) custom-call(s32[1]{0:T(128)} %bitcast.index_ref, f32[128,1,256]{2,1,0:T(1,128)S(1)} %all-to-all-done.1.take_ref, f32[10,16,1024]{2,1,0:T(8,128)S(1)} %get-tuple-element.13.part_ref, f32[16]{0:T(128)S(1)} %copy-done.18, f32[1,1024]{1,0:T(1,128)S(1)} %copy-done.15, ...), custom_call_target="tpu_custom_call" | custom-call | flops 2013265920 | bytes 10485760 | tf_op jit(solution)/shard_map/pallas_call | solution.py:287
  (17 shorter events, 0.1 us)
Async XLA Ops:
  0.6 51.2 %copy-start.15 = (f32[1,1024]{1,0:T(1,128)S(1)}, f32[1,1024]{1,0:T(1,128)}, u32[]{:S(2)}) copy-start(f32[1,1024]{1,0:T(1,128)} %constant.30.eigen_ref) | copy-start | bytes 12292
  0.6 1.0 %copy-start.4 = (f32[16,8,1024]{2,1,0:T(8,128)S(1)}, f32[16,8,1024]{2,1,0:T(8,128)}, u32[]{:S(2)}) copy-start(f32[16,8,1024]{2,1,0:T(8,128)} %vortex_ref.3) | copy-start | bytes 1572868
  1.7 0.7 copy-start.14
  2.4 0.7 copy-start.17
  3.0 0.7 %copy-start.20 = (f32[16,16]{1,0:T(8,128)S(1)}, f32[16,16]{1,0:T(8,128)}, u32[]{:S(2)}) copy-start(f32[16,16]{1,0:T(8,128)} %mix_ref.2) | copy-start | bytes 3076
  3.7 0.9 %copy-start.21 = (f32[32,1024]{1,0:T(8,128)S(1)}, f32[32,1024]{1,0:T(8,128)}, u32[]{:S(2)}) copy-start(f32[32,1024]{1,0:T(8,128)} %constant.24.clone.cb_ref) | copy-start | bytes 393220
  4.6 0.9 %copy-start.22 = (f32[32,1024]{1,0:T(8,128)S(1)}, f32[32,1024]{1,0:T(8,128)}, u32[]{:S(2)}) copy-start(f32[32,1024]{1,0:T(8,128)} %constant.23.clone.sb_ref) | copy-start | bytes 393220
  5.5 0.9 %copy-start.23 = (f32[32,1024]{1,0:T(8,128)S(1)}, f32[32,1024]{1,0:T(8,128)}, u32[]{:S(2)}) copy-start(f32[32,1024]{1,0:T(8,128)} %constant.22.clone.ca_ref) | copy-start | bytes 393220
  6.4 0.9 %copy-start.24 = (f32[32,1024]{1,0:T(8,128)S(1)}, f32[32,1024]{1,0:T(8,128)}, u32[]{:S(2)}) copy-start(f32[32,1024]{1,0:T(8,128)} %constant.21.clone.sa_ref) | copy-start | bytes 393220
  7.4 22.6 %copy-start.18 = (f32[16]{0:T(128)S(1)}, f32[16]{0:T(128)}, u32[]{:S(2)}) copy-start(f32[16]{0:T(128)} %radii_ref.7) | copy-start | bytes 196
  7.4 22.6 %copy-start.19 = (f32[8,128]{1,0:T(8,128)S(1)}, f32[8,128]{1,0:T(8,128)}, u32[]{:S(2)}) copy-start(f32[8,128]{1,0:T(8,128)} %constant.29.eigen_ref) | copy-start | bytes 12292
  7.4 31.9 %copy-start.5 = (f32[16,8,1024]{2,1,0:T(8,128)S(1)}, f32[16,8,1024]{2,1,0:T(8,128)}, u32[]{:S(2)}) copy-start(f32[16,8,1024]{2,1,0:T(8,128)} %vortex_ref.3) | copy-start | bytes 1572868
  7.4 44.5 %copy-start.12 = (f32[8,1024]{1,0:T(8,128)S(1)}, f32[8,1024]{1,0:T(8,128)}, u32[]{:S(2)}) copy-start(f32[8,1024]{1,0:T(8,128)} %wind_ref.1) | copy-start | bytes 98308
  7.4 44.5 %copy-start.13 = (s32[8,1024]{1,0:T(8,128)S(1)}, s32[8,1024]{1,0:T(8,128)}, u32[]{:S(2)}) copy-start(s32[8,1024]{1,0:T(8,128)} %wet_ref.1) | copy-start | bytes 98308
  7.4 44.5 %copy-start.16 = (f32[16,16]{1,0:T(8,128)S(1)}, f32[16,16]{1,0:T(8,128)}, u32[]{:S(2)}) copy-start(f32[16,16]{1,0:T(8,128)} %mix_ref.3) | copy-start | bytes 3076
  10.7 1.4 %copy-start.2 = (bf16[1024,1024]{1,0:T(8,128)(2,1)}, bf16[1024,1024]{1,0:T(8,128)(2,1)S(1)}, u32[]{:S(2)}) copy-start(bf16[1024,1024]{1,0:T(8,128)(2,1)S(1)} %get-tuple-element.15.low_ref) | copy-start | bytes 6291460
  12.1 0.8 %copy-start.8 = (f32[8,16,1024]{2,1,0:T(8,128)}, f32[8,16,1024]{2,1,0:T(8,128)S(1)}, u32[]{:S(2)}) copy-start(f32[8,16,1024]{2,1,0:T(8,128)S(1)} %get-tuple-element.12.force_ref) | copy-start | bytes 1572868
  12.9 17.1 %all-to-all-start = ((f32[128,1,256]{2,1,0:T(1,128)}), f32[128,1,256]{2,1,0:T(1,128)S(1)}, u32[]{:S(2)}, u32[]{:S(2)}) async-start(f32[128,1,256]{2,1,0:T(1,128)} %get-tuple-element.11), calls=%async_computation | async-start | bytes 262144 | tf_op jit(solution)/shard_map/all_to_all | solution.py:313
  31.7 27.9 %all-to-all-start.1 = ((f32[128,1,256]{2,1,0:T(1,128)}), f32[128,1,256]{2,1,0:T(1,128)S(1)}, u32[]{:S(2)}, u32[]{:S(2)}) async-start(f32[128,1,256]{2,1,0:T(1,128)} %shard_map.123), calls=%async_computation.1 | async-start | bytes 262144 | tf_op jit(solution)/shard_map/all_to_all | solution.py:328
  39.4 5.8 %collective-permute-start = (f32[16,1024]{1,0:T(8,128)S(1)}, f32[16,1024]{1,0:T(8,128)S(1)}, u32[]{:S(2)}, u32[]{:S(2)}) collective-permute-start(f32[16,1024]{1,0:T(8,128)S(1)} %bitcast.7), channel_id=1, source_target_pairs={{0,1},{1,2},{2,3},{3,4},{4,5},{5,6},{6,7},{7,8},{8,9},{9,10},{10,1... | collective-permute-start | bytes 196616 | tf_op jit(solution)/shard_map/ppermute | solution.py:303
  43.2 8.6 %collective-permute-start.1 = (f32[16,1024]{1,0:T(8,128)S(1)}, f32[16,1024]{1,0:T(8,128)S(1)}, u32[]{:S(2)}, u32[]{:S(2)}) collective-permute-start(f32[16,1024]{1,0:T(8,128)S(1)} %bitcast.8), channel_id=1, source_target_pairs={{1,0},{2,1},{3,2},{4,3},{5,4},{6,5},{7,6},{8,7},{9,8},{10,9},{11,1... | collective-permute-start | bytes 196616 | tf_op jit(solution)/shard_map/ppermute | solution.py:304
  51.9 1.0 %copy-start.9 = (f32[8,16,1024]{2,1,0:T(8,128)S(1)}, f32[8,16,1024]{2,1,0:T(8,128)}, u32[]{:S(2)}) copy-start(f32[8,16,1024]{2,1,0:T(8,128)} %copy-done.8) | copy-start | bytes 1572868
  56.2 2.0 %copy-start = (f32[8,16,8,1024]{3,2,1,0:T(8,128)}, f32[8,16,8,1024]{3,2,1,0:T(8,128)S(1)}, u32[]{:S(2)}) copy-start(f32[8,16,8,1024]{3,2,1,0:T(8,128)S(1)} %get-tuple-element.18.coef_ref) | copy-start | bytes 12582916
  58.1 0.8 %copy-start.6 = (f32[16,8,1024]{2,1,0:T(8,128)}, f32[16,8,1024]{2,1,0:T(8,128)S(1)}, u32[]{:S(2)}) copy-start(f32[16,8,1024]{2,1,0:T(8,128)S(1)} %get-tuple-element.17.base_ref) | copy-start | bytes 1572868
  58.9 0.7 copy-start.10
  59.6 2.2 %copy-start.1 = (f32[8,16,8,1024]{3,2,1,0:T(8,128)S(1)}, f32[8,16,8,1024]{3,2,1,0:T(8,128)}, u32[]{:S(2)}) copy-start(f32[8,16,8,1024]{3,2,1,0:T(8,128)} %copy-done) | copy-start | bytes 12582916
  61.8 1.6 %copy-start.3 = (bf16[1024,1024]{1,0:T(8,128)(2,1)S(1)}, bf16[1024,1024]{1,0:T(8,128)(2,1)}, u32[]{:S(2)}) copy-start(bf16[1024,1024]{1,0:T(8,128)(2,1)} %copy-done.2) | copy-start | bytes 6291460
  63.4 1.0 %copy-start.7 = (f32[16,8,1024]{2,1,0:T(8,128)S(1)}, f32[16,8,1024]{2,1,0:T(8,128)}, u32[]{:S(2)}) copy-start(f32[16,8,1024]{2,1,0:T(8,128)} %copy-done.6) | copy-start | bytes 1572868
  64.4 0.9 %copy-start.11 = (f32[160,160]{1,0:T(8,128)S(1)}, f32[160,160]{1,0:T(8,128)}, u32[]{:S(2)}) copy-start(f32[160,160]{1,0:T(8,128)} %copy-done.10) | copy-start | bytes 307204
where the time goes:
time: 69.8 us; the launch traced here: 69.2 us
  starting transfers between devices  23.8 us (34%)
  local copies, waits for them, and re-layouts  19.2 us (28%)
  waiting for transfers between devices  13.2 us (19%)
  Pallas kernels  12.2 us (17%)
  between operations  0.8 us (1%)
    unnamed x52, local copies, waits for them, and re-layouts  19.1 us
    pallas_call x4, Pallas kernels, call(): pl.pallas_call(kernel, out_shape=[jax.ShapeDtypeStruct(s, d) for s, d in...  12.2 us
    all_to_all x1, starting transfers between devices, body(): take = lax.all_to_all(send, AXES, split_axis=0, concat_axis=0, tiled=True)  10.5 us
    all_to_all x1, starting transfers between devices, body(): lax.all_to_all(give, AXES, split_axis=0, concat_axis=0, tiled=True)  7.55 us
    ppermute x1, waiting for transfers between devices, body(): lax.ppermute(vorticity[:, 0], AXES, [(i + 1, i) for i in range(BLOCKS - 1)])  6.65 us
    all_to_all x1, waiting for transfers between devices, body(): take = lax.all_to_all(send, AXES, split_axis=0, concat_axis=0, tiled=True)  6.59 us
    ppermute x1, starting transfers between devices, body(): lax.ppermute(vorticity[:, ROWS - 1], AXES, [(i, i + 1) for i in range(BLO...  3.81 us
    ppermute x1, starting transfers between devices, body(): lax.ppermute(vorticity[:, 0], AXES, [(i + 1, i) for i in range(BLOCKS - 1)])  1.92 us
  transfers between devices with their start and end apart: 4, of which 2 were waited for; matrix products, arithmetic and copies ran while one was open for 0% of the time, Pallas kernels for 5%

commit v1 on v0

v1 whole, which is shorter than its diff:
```python
import math

import jax
import jax.numpy as jnp
import numpy as np
from jax import lax
from jax.experimental import pallas as pl
from jax.experimental.pallas import tpu as pltpu
from jax.sharding import PartitionSpec as P

time_step = 0.5
beta_plane = 1.0
bottom_drag = 0.2

N = 1024
NL = 16
ROWS = 8
TALL = ROWS + 2
BLOCKS = 128
LANES = 128
STEP = 256
PIECES = N // STEP
AXES = ("group", "tile")
HIGHEST = lax.Precision.HIGHEST
SMEM = pl.BlockSpec(memory_space=pltpu.SMEM)
ANY = pl.BlockSpec(memory_space=pl.ANY)
DMA = pltpu.SemaphoreType.DMA
f32, bf16, i32 = jnp.float32, jnp.bfloat16, jnp.int32


def host_table():
    k = np.arange(1, N + 1)
    turn = 2 * (N + 1)
    angle_a = np.pi * ((32 * np.arange(32)[:, None] * k[None, :]) % turn) / (N + 1)
    angle_b = np.pi * ((np.arange(1, 33)[:, None] * k[None, :]) % turn) / (N + 1)
    scale = math.sqrt(2.0 / (N + 1))
    table = [np.sin(angle_a), np.cos(angle_a), scale * np.sin(angle_b), scale * np.cos(angle_b)]
    return np.stack(table).astype(np.float32)


def iota(shape, dim):
    return lax.broadcasted_iota(jnp.int32, shape, dim)


def dot(left, right, precision=None):
    return lax.dot_general(
        left, right, (((1,), (0,)), ((), ())), precision=precision, preferred_element_type=jnp.float32
    )


def halves(value):
    high = value.astype(jnp.bfloat16)
    low = (value - high.astype(jnp.float32)).astype(jnp.bfloat16)
    return high, low


def split_dot(left, right):
    count = left[0].shape[0]
    both = dot(jnp.concatenate(left, 0), right[0])
    return both[:count] + both[count:] + dot(left[0], right[1])


def fetch(pairs, sems, first=0):
    copies = [pltpu.make_async_copy(src, dst, sems.at[first + i]) for i, (src, dst) in enumerate(pairs)]
    for copy in copies:
        copy.start()
    return copies


def wait(copies):
    for copy in copies:
        copy.wait()


def eigen_values(first, width):
    wave = (iota((1, width), 1) + (first + 1)).astype(jnp.float32)
    angle = wave * (math.pi / (2 * (N + 1)))
    square = angle * angle
    series = jnp.full_like(square, 1.0 / math.factorial(15))
    for order in (13, 11, 9, 7, 5, 3, 1):
        series = 1.0 / math.factorial(order) - square * series
    sine = angle * series
    return 4.0 * sine * sine


def radii_column(radii_ref, shape):
    sub = iota(shape, 0)
    column = jnp.zeros(shape, jnp.float32)
    for m in range(NL):
        column = jnp.where(sub == m, radii_ref[m], column)
    return column


def decay_of(shift):
    half = 0.5 * jnp.sqrt(shift)
    root = jnp.sqrt(1.0 + 0.25 * shift)
    grow = half + root
    return 1.0 / (grow * grow), 1.0 / (4.0 * half * root)


def mode_decay(radii_ref):
    return decay_of(eigen_values(0, N) + radii_column(radii_ref, (NL, N)))


def forward_kernel(
    vortex_hbm, mix_hbm, radii_hbm, table_hbm,
    send_hbm, force_hbm, first_hbm, last_hbm, high_hbm, low_hbm,
    vortex_ref, mix_ref, radii_ref, table_ref,
    send_ref, force_ref, first_ref, last_ref, high_ref, low_ref, sems,
):
    copies = fetch(
        [(mix_hbm, mix_ref), (radii_hbm, radii_ref), (vortex_hbm, vortex_ref), (table_hbm, table_ref)], sems
    )
    rows = NL * ROWS
    spread = (iota((NL, rows), 1) // ROWS == iota((NL, rows), 0)).astype(jnp.float32)
    wait(copies[:2])
    rho, weight = mode_decay(radii_ref)
    wide = dot(mix_ref[...], spread, HIGHEST)
    mix = jnp.concatenate([wide] * ROWS, 0)
    mix = jnp.where(iota((rows, rows), 0) // NL == iota((rows, rows), 1) % ROWS, mix, 0.0)
    wait(copies[2:3])
    first_ref[...] = vortex_ref[:, 0]
    last_ref[...] = vortex_ref[:, ROWS - 1]
    written = fetch([(first_ref, first_hbm), (last_ref, last_hbm)], sems, 4)
    modal = split_dot(halves(mix), halves(vortex_ref[...].reshape(rows, N)))
    split = halves(modal)
    wait(copies[3:])
    for n in range(PIECES):
        cols = slice(n * STEP, (n + 1) * STEP)
        for a in range(32):
            block = table_ref[0, a : a + 1, cols] * table_ref[3, :, cols]
            block += table_ref[1, a : a + 1, cols] * table_ref[2, :, cols]
            high, low = halves(block)
            high_ref[n, 32 * a : 32 * a + 32] = high
            low_ref[n, 32 * a : 32 * a + 32] = low
        written += fetch([(high_ref.at[n], high_hbm.at[n]), (low_ref.at[n], low_hbm.at[n])], sems, 6 + 3 * n)
        spectrum = split_dot(split, (high_ref[n], low_ref[n]))
        right = jnp.zeros((NL, STEP), jnp.float32)
        left = jnp.zeros((NL, STEP), jnp.float32)
        force = []
        for y in range(ROWS):
            force.append(-weight[:, cols] * spectrum[y * NL : (y + 1) * NL])
            force_ref[y, :, cols] = force[y]
            right = rho[:, cols] * right + force[y]
        for y in reversed(range(ROWS)):
            left = rho[:, cols] * left + force[y]
        for c in range(STEP // LANES):
            dest = n * (STEP // LANES) + c
            part = slice(c * LANES, (c + 1) * LANES)
            send_ref[dest * NL : (dest + 1) * NL, 0, :LANES] = right[:, part]
            send_ref[dest * NL : (dest + 1) * NL, 0, LANES:] = left[:, part]
        dests = pl.ds(n * (STEP // LANES) * NL, STEP // LANES * NL)
        written += fetch([(send_ref.at[dests], send_hbm.at[dests])], sems, 8 + 3 * n)
    written += fetch([(force_ref, force_hbm)], sems, 6 + 3 * PIECES)
    wait(written)


def shift_rows(value, step):
    blank = jnp.zeros((abs(step), value.shape[1]), value.dtype)
    if step > 0:
        return jnp.concatenate([blank, value[:-step]], 0)
    return jnp.concatenate([value[-step:], blank], 0)


def scan_kernel(
    index_ref, radii_hbm, take_hbm, after_hbm, first_hbm, last_hbm, give_hbm, radii_ref, take_ref, give_ref, sems
):
    del after_hbm, first_hbm, last_hbm
    copies = fetch([(radii_hbm, radii_ref), (take_hbm, take_ref)], sems)
    copies[0].wait()
    me = index_ref[0]
    rho, _ = decay_of(eigen_values(me // NL * LANES, LANES) + radii_ref[me % NL])
    rho2 = rho * rho
    rho4 = rho2 * rho2
    place = iota((BLOCKS, LANES), 0)
    rates = [rho4 * rho4]
    while 2 ** len(rates) <= BLOCKS:
        rates.append(rates[-1] * rates[-1])
    power = jnp.ones((BLOCKS, LANES), jnp.float32)
    reverse = power
    for bit, rate in enumerate(rates[:-1]):
        odd = (place >> bit) % 2 == 1
        power = power * jnp.where(odd, rate, 1.0)
        reverse = reverse * jnp.where(odd, 1.0, rate)
    copies[1].wait()
    right = take_ref[:, 0, :LANES]
    left = take_ref[:, 0, LANES:]
    for bit, rate in enumerate(rates[:-1]):
        right = right + rate * shift_rows(right, 1 << bit)
        left = left + rate * shift_rows(left, -1 << bit)
    below = rho * left[:1]
    above = rho * right[BLOCKS - 1 :]
    far = rates[-1] * rho
    scale = 1.0 / (1.0 - far * far)
    alpha = -(below - far * above) * scale
    beta = -(above - far * below) * scale
    give_ref[:, 0, :LANES] = shift_rows(right, 1) + alpha * power
    give_ref[:, 0, LANES:] = shift_rows(left, -1) + beta * reverse
    wait(fetch([(give_ref, give_hbm)], sems))


def part_kernel(
    force_hbm, radii_hbm, mix_hbm, part_hbm, mixed_hbm, force_ref, radii_ref, mix_ref, part_ref, mixed_ref, sems
):
    copies = fetch([(radii_hbm, radii_ref), (mix_hbm, mix_ref), (force_hbm, force_ref)], sems)
    wait(copies[:2])
    tall = NL * TALL
    row = iota((tall, NL), 0)
    layer = jnp.where(row < NL * ROWS, row // ROWS, row % NL)
    pick = (layer == iota((tall, NL), 1)).astype(jnp.float32)
    wide = (iota((NL, tall), 1) % NL == iota((NL, tall), 0)).astype(jnp.float32)
    mixed = dot(dot(pick, mix_ref[...], HIGHEST), wide, HIGHEST)
    row = iota((tall, tall), 0)
    place = jnp.where(row < NL * ROWS, row % ROWS + 1, jnp.where(row < NL * (ROWS + 1), 0, ROWS + 1))
    mixed_ref[...] = jnp.where(iota((tall, tall), 1) // NL == place, mixed, 0.0)
    written = fetch([(mixed_ref, mixed_hbm)], sems, 3)
    rho, _ = mode_decay(radii_ref)
    wait(copies[2:])
    right = jnp.zeros((NL, N), jnp.float32)
    for y in range(ROWS):
        right = rho * right + force_ref[y]
        part_ref[y + 1] = right
    part_ref[ROWS + 1] = rho * right
    left = jnp.zeros((NL, N), jnp.float32)
    for y in reversed(range(ROWS)):
        part_ref[y + 1] += left
        left = rho * (left + force_ref[y])
    part_ref[0] = left
    wait(written + fetch([(part_ref, part_hbm)], sems, 4))


def roll_lanes(value, step):
    width = value.shape[1]
    lane = iota(value.shape, 1)
    rolled = pltpu.roll(value, step % width, 1)
    return jnp.where(lane == (0 if step > 0 else width - 1), 0.0, rolled)


def roll_sub(value, edge, step):
    height = value.shape[0]
    sub = iota(value.shape, 0)
    rolled = pltpu.roll(value, step % height, 0)
    return jnp.where(sub == (0 if step > 0 else height - 1), edge, rolled)


def weight_kernel(
    vortex_hbm, wind_hbm, wet_hbm, south_hbm, north_hbm, after_hbm, base_hbm, coef_hbm, drag_hbm,
    vortex_ref, wind_ref, wet_ref, south_ref, north_ref, base_ref, coef_ref, drag_ref, sems,
):
    del after_hbm
    wait(
        fetch(
            [
                (wet_hbm, wet_ref), (wind_hbm, wind_ref), (south_hbm, south_ref), (north_hbm, north_ref),
                (vortex_hbm, vortex_ref),
            ],
            sems,
        )
    )
    keep = time_step * wet_ref[...].astype(jnp.float32)
    twelfth = keep * (1.0 / 12.0)
    written = []
    for layer in range(NL):
        mid = vortex_ref[layer]
        north = roll_sub(mid, north_ref[layer : layer + 1], -1)
        south = roll_sub(mid, south_ref[layer : layer + 1], 1)
        east = roll_lanes(mid, -1)
        west = roll_lanes(mid, 1)
        north_east = roll_lanes(north, -1)
        north_west = roll_lanes(north, 1)
        south_east = roll_lanes(south, -1)
        south_west = roll_lanes(south, 1)
        along = north - south
        across = east - west
        c_east = -twelfth * (along + (north_east - south_east)) - keep * (0.5 * beta_plane)
        c_west = twelfth * (along + (north_west - south_west)) + keep * (0.5 * beta_plane)
        c_north = twelfth * (across + (north_east - north_west))
        c_south = -twelfth * (across + (south_east - south_west))
        if layer == NL - 1:
            drag = keep * bottom_drag
            c_east = c_east - drag
            c_west = c_west - drag
            c_north = c_north - drag
            c_south = c_south - drag
            drag_ref[...] = 4.0 * drag
        coef_ref[layer, 0] = c_north
        coef_ref[layer, 1] = c_south
        coef_ref[layer, 2] = roll_lanes(c_east, 1)
        coef_ref[layer, 3] = roll_lanes(-twelfth * (north - east), 1)
        coef_ref[layer, 4] = roll_lanes(twelfth * (south - east), 1)
        coef_ref[layer, 5] = roll_lanes(c_west, -1)
        coef_ref[layer, 6] = roll_lanes(twelfth * (north - west), -1)
        coef_ref[layer, 7] = roll_lanes(-twelfth * (south - west), -1)
        base_ref[layer] = mid + keep * wind_ref[...] if layer == 0 else mid
        if layer % 4 == 3:
            some = pl.ds(layer - 3, 4)
            written += fetch([(coef_ref.at[some], coef_hbm.at[some])], sems, 5 + layer // 4)
    wait(written + fetch([(base_ref, base_hbm), (drag_ref, drag_hbm)], sems, 9))


def backward_kernel(
    index_ref, radii_hbm, take_hbm, part_hbm, mixed_hbm, high_hbm, low_hbm, base_hbm, coef_hbm, drag_hbm,
    vortex_hbm, stream_hbm,
    radii_ref, take_ref, part_ref, mixed_ref, high_ref, low_ref, base_ref, coef_ref, drag_ref,
    psi_ref, wave_ref, vortex_ref, stream_ref, sems,
):
    copies = fetch(
        [
            (radii_hbm, radii_ref), (take_hbm, take_ref), (part_hbm, part_ref), (mixed_hbm, mixed_ref),
            (high_hbm, high_ref), (low_hbm, low_ref), (coef_hbm, coef_ref), (base_hbm, base_ref),
            (drag_hbm, drag_ref),
        ],
        sems,
    )
    out = len(copies)
    copies[0].wait()
    rho, _ = mode_decay(radii_ref)
    wait(copies[1:3])
    for c in range(N // LANES):
        cols = slice(c * LANES, (c + 1) * LANES)
        up = take_ref[c * NL : (c + 1) * NL, 0, :LANES]
        down = take_ref[c * NL : (c + 1) * NL, 0, LANES:]
        near = rho[:, cols]
        ups, downs = [up], [down]
        for _ in range(ROWS + 1):
            ups.append(ups[-1] * near)
            downs.append(downs[-1] * near)
        for i in range(TALL):
            psi_ref[i * NL : (i + 1) * NL, cols] = part_ref[i, :, cols] + ups[i] + downs[ROWS + 1 - i]
    wait(copies[3:4])
    split = halves(split_dot(halves(mixed_ref[...]), halves(psi_ref[...])))
    wait(copies[4:6])
    for n in range(PIECES):
        wave_ref[:, n * STEP : (n + 1) * STEP] = split_dot(split, (high_ref[n], low_ref[n]))
    inside_low = jnp.where(index_ref[0] > 0, 1.0, 0.0)
    inside_high = jnp.where(index_ref[0] < BLOCKS - 1, 1.0, 0.0)
    body = NL * ROWS
    for layer in range(NL):
        stream_ref[layer] = wave_ref[layer * ROWS : (layer + 1) * ROWS]
    written = fetch([(stream_ref, stream_hbm)], sems, out)
    wait(copies[6:])
    for layer in range(NL):
        mid = wave_ref[layer * ROWS : (layer + 1) * ROWS]
        north = roll_sub(mid, inside_high * wave_ref[body + NL + layer : body + NL + layer + 1], -1)
        south = roll_sub(mid, inside_low * wave_ref[body + layer : body + layer + 1], 1)
        total = base_ref[layer] + coef_ref[layer, 0] * north + coef_ref[layer, 1] * south
        if layer == NL - 1:
            total = total + drag_ref[...] * mid
        from_east = coef_ref[layer, 2] * mid + coef_ref[layer, 3] * north + coef_ref[layer, 4] * south
        from_west = coef_ref[layer, 5] * mid + coef_ref[layer, 6] * north + coef_ref[layer, 7] * south
        vortex_ref[layer] = total + pltpu.roll(from_east, N - 1, 1) + pltpu.roll(from_west, 1, 1)
        if layer % 4 == 3:
            some = pl.ds(layer - 3, 4)
            written += fetch([(vortex_ref.at[some], vortex_hbm.at[some])], sems, out + 1 + layer // 4)
    wait(written)


def call(kernel, outs, args, scratch, flops, nbytes, index=None, limit=60 * 1024 * 1024):
    def room(kind):
        return pltpu.VMEM(*kind) if isinstance(kind, tuple) else kind

    lead = [] if index is None else [index]
    return pl.pallas_call(
        kernel,
        out_shape=[jax.ShapeDtypeStruct(s, d) for s, d in outs],
        in_specs=[SMEM] * len(lead) + [ANY] * len(args),
        out_specs=[ANY] * len(outs),
        scratch_shapes=[room(kind) for kind in scratch],
        compiler_params=pltpu.CompilerParams(vmem_limit_bytes=limit),
        cost_estimate=pl.CostEstimate(flops=flops, bytes_accessed=nbytes, transcendentals=0),
    )(*lead, *args)


def body(vorticity, layer_to_mode, mode_to_layer, inverse_radii, wind_curl, wet_mask):
    field = ((NL, ROWS, N), f32)
    plane = ((ROWS, N), f32)
    edge = ((NL, N), f32)
    mixing = ((NL, NL), f32)
    sines = ((PIECES, N, STEP), bf16)
    packet = ((BLOCKS, 1, 2 * LANES), f32)
    rows = ((ROWS, NL, N), f32)
    rates = pltpu.SMEM((NL,), f32)
    parts = [((TALL, NL, N), f32), ((NL * TALL, NL * TALL), f32)]
    weights = [field, ((NL, 8, ROWS, N), f32), plane]
    wave = ((NL * TALL, N), f32)

    index = (lax.axis_index("group") * lax.axis_size("tile") + lax.axis_index("tile")).astype(i32).reshape(1)
    outs = [packet, rows, edge, edge, sines, sines]
    send, force, first, last, high, low = call(
        forward_kernel, outs, (vorticity, layer_to_mode, inverse_radii, jnp.asarray(host_table())),
        [field, mixing, rates, ((4, 32, N), f32), *outs, DMA((7 + 3 * PIECES,))],
        6 * 128 * N * N, 6 << 20,
    )
    take = lax.all_to_all(send, AXES, split_axis=0, concat_axis=0, tiled=True)
    south = lax.ppermute(last, AXES, [(i, i + 1) for i in range(BLOCKS - 1)])
    north = lax.ppermute(first, AXES, [(i + 1, i) for i in range(BLOCKS - 1)])
    part, mixed = call(
        part_kernel, parts, (force, inverse_radii, mode_to_layer), [rows, rates, mixing, *parts, DMA((5,))],
        1 << 24, 1 << 20,
    )
    (give,) = call(
        scan_kernel, [packet], (inverse_radii, take, part, south, north), [rates, packet, packet, DMA((2,))],
        1 << 22, 1 << 18, index,
    )
    amplitude = lax.all_to_all(give, AXES, split_axis=0, concat_axis=0, tiled=True)
    base, coef, drag = call(
        weight_kernel, weights, (vorticity, wind_curl, wet_mask, south, north, give),
        [field, plane, ((ROWS, N), i32), edge, edge, *weights, DMA((11,))],
        1 << 24, 5 << 20,
    )
    return tuple(
        call(
            backward_kernel, [field, field],
            (inverse_radii, amplitude, part, mixed, high, low, base, coef, drag),
            [rates, packet, *parts, sines, sines, *weights, wave, wave, field, field, DMA((14,))],
            6 * 160 * N * N, 10 << 20, index,
        )
    )


def solution(mesh):
    rows = P(None, AXES, None)
    return jax.shard_map(
        body,
        mesh=mesh,
        in_specs=(rows, P(), P(), P(), P(AXES, None), P(AXES, None)),
        out_specs=(rows, rows),
        check_vma=False,
    )
```

time: 69.8 us -> 56.6 us (0.81)
  the two profiles are of different devices: /device:TPU:31 before, /device:TPU:1 now
where the time goes in v1:
time: 56.6 us; the launch traced here: 56.3 us
  starting transfers between devices  28.1 us (50%)
  Pallas kernels  18.6 us (33%)
  waiting for transfers between devices  7.56 us (13%)
  local copies, waits for them, and re-layouts  1.31 us (2%)
  between operations  0.72 us (1%)
    pallas_call x5, Pallas kernels, call(): pl.pallas_call(kernel, out_shape=[jax.ShapeDtypeStruct(s, d) for s, d in...  18.6 us
    all_to_all x1, starting transfers between devices, body(): take = lax.all_to_all(send, AXES, split_axis=0, concat_axis=0, tiled=True)  11.5 us
    all_to_all x1, starting transfers between devices, body(): lax.all_to_all(give, AXES, split_axis=0, concat_axis=0, tiled=True)  11.1 us
    all_to_all x1, waiting for transfers between devices, body(): lax.all_to_all(give, AXES, split_axis=0, concat_axis=0, tiled=True)  5.16 us
    ppermute x1, starting transfers between devices, body(): south = lax.ppermute(last, AXES, [(i, i + 1) for i in range(BLOCKS - 1)])  3.54 us
    ppermute x1, starting transfers between devices, body(): north = lax.ppermute(first, AXES, [(i + 1, i) for i in range(BLOCKS - 1)])  1.92 us
    ppermute x1, waiting for transfers between devices, body(): north = lax.ppermute(first, AXES, [(i + 1, i) for i in range(BLOCKS - 1)])  1.81 us
    unnamed x8, local copies, waits for them, and re-layouts  1.31 us
  transfers between devices with their start and end apart: 4, of which 3 were waited for; matrix products, arithmetic and copies ran while one was open for 0% of the time, Pallas kernels for 13%

profile of v1, /device:TPU:1, one launch (start us, length us, event | category | flops | bytes accessed | tf_op | source)
XLA Modules:
  0.0 56.3 jit_solution(18153001318594410564)
XLA Ops:
  0.6 4.3 %shard_map.86 = (f32[128,1,256]{2,1,0:T(1,128)}, f32[8,16,1024]{2,1,0:T(8,128)}, f32[16,1024]{1,0:T(8,128)}, f32[16,1024]{1,0:T(8,128)}, bf16[4,1024,256]{2,1,0:T(8,128)(2,1)}, /*index=5*/bf16[4,1024,256]{2,1,0:T(8,128)(2,1)}) custom-call(f32[16,8,1024]{2,1,0:T(8,128)} %vortex_hbm.3, f32[16,16]{1,0:T(8,128)} %mix_hbm.2, f32[16]{0:T(128)} %radii_hbm.7, ...), custom_call_target="tpu_custom_call" | custom-call | flops 805306368 | bytes 6291456 | tf_op jit(solution)/shard_map/pallas_call | solution.py:363
  5.0 11.5 %all-to-all-start = ((f32[128,1,256]{2,1,0:T(1,128)}), f32[128,1,256]{2,1,0:T(1,128)S(1)}, u32[]{:S(2)}, u32[]{:S(2)}) async-start(f32[128,1,256]{2,1,0:T(1,128)} %get-tuple-element.13), calls=%async_computation | async-start | bytes 262144 | tf_op jit(solution)/shard_map/all_to_all | solution.py:394
  16.5 3.5 %collective-permute-start = (f32[16,1024]{1,0:T(8,128)}, f32[16,1024]{1,0:T(8,128)S(1)}, u32[]{:S(2)}, u32[]{:S(2)}) collective-permute-start(f32[16,1024]{1,0:T(8,128)} %get-tuple-element.16), channel_id=1, source_target_pairs={{0,1},{1,2},{2,3},{3,4},{4,5},{5,6},{6,7},{7,8},{8,9},{9,10},{10,1... | collective-permute-start | bytes 196616 | tf_op jit(solution)/shard_map/ppermute | solution.py:395
  20.0 1.9 %collective-permute-start.1 = (f32[16,1024]{1,0:T(8,128)}, f32[16,1024]{1,0:T(8,128)S(1)}, u32[]{:S(2)}, u32[]{:S(2)}) collective-permute-start(f32[16,1024]{1,0:T(8,128)} %get-tuple-element.17), channel_id=1, source_target_pairs={{1,0},{2,1},{3,2},{4,3},{5,4},{6,5},{7,6},{8,7},{9,8},{10,9},{11,1... | collective-permute-start | bytes 196616 | tf_op jit(solution)/shard_map/ppermute | solution.py:396
  21.9 2.3 %shard_map.87 = (f32[10,16,1024]{2,1,0:T(8,128)}, f32[160,160]{1,0:T(8,128)}) custom-call(f32[8,16,1024]{2,1,0:T(8,128)} %get-tuple-element.14.force_hbm, f32[16]{0:T(128)} %radii_hbm.7, f32[16,16]{1,0:T(8,128)} %mix_hbm.3), custom_call_target="tpu_custom_call" | custom-call | flops 16777216 | bytes 1048576 | tf_op jit(solution)/shard_map/pallas_call | solution.py:363
  24.3 0.0 collective-permute-done.first_hbm.south_hbm
  24.3 0.0 copy-start.2
  24.3 1.8 %collective-permute-done.1.last_hbm.north_hbm = f32[16,1024]{1,0:T(8,128)S(1)} collective-permute-done((f32[16,1024]{1,0:T(8,128)}, f32[16,1024]{1,0:T(8,128)S(1)}, u32[]{:S(2)}, u32[]{:S(2)}) %collective-permute-start.1) | collective-permute-done | bytes 65568 | tf_op jit(solution)/shard_map/ppermute | solution.py:396
  26.1 0.0 copy-start.3
  26.1 0.6 %all-to-all-done.take_hbm = f32[128,1,256]{2,1,0:T(1,128)S(1)} async-done(((f32[128,1,256]{2,1,0:T(1,128)}), f32[128,1,256]{2,1,0:T(1,128)S(1)}, u32[]{:S(2)}, u32[]{:S(2)}) %all-to-all-start) | async-done | bytes 131104 | tf_op jit(solution)/shard_map/all_to_all | solution.py:394
  26.7 0.0 copy-start.1
  26.7 0.0 copy-done.2
  26.7 0.0 copy-done.3
  26.7 0.6 %copy-done.1 = f32[128,1,256]{2,1,0:T(1,128)} copy-done((f32[128,1,256]{2,1,0:T(1,128)}, f32[128,1,256]{2,1,0:T(1,128)S(1)}, u32[]{:S(2)}) %copy-start.1) | copy-done | bytes 131096
  27.3 1.9 %shard_map.88.after_hbm = f32[128,1,256]{2,1,0:T(1,128)} custom-call(s32[1]{0:T(128)} %bitcast.index_ref, f32[16]{0:T(128)} %radii_hbm.7, f32[128,1,256]{2,1,0:T(1,128)} %copy-done.1, f32[10,16,1024]{2,1,0:T(8,128)} %get-tuple-element.15.after_hbm.part_hbm, f32[16,1024]{1,0:T(8,128)} %copy-done.2, f32[16,1024]{1,0:T(8,128)} %copy-done.3), custom_call_target="tpu_custom_call" | custom-call | flops 4194304 | bytes 262144 | tf_op jit(solution)/shard_map/pallas_call | solution.py:363
  29.2 11.1 %all-to-all-start.1 = ((f32[128,1,256]{2,1,0:T(1,128)}), f32[128,1,256]{2,1,0:T(1,128)S(1)}, u32[]{:S(2)}, u32[]{:S(2)}) async-start(f32[128,1,256]{2,1,0:T(1,128)} %shard_map.88.after_hbm), calls=%async_computation.1 | async-start | bytes 262144 | tf_op jit(solution)/shard_map/all_to_all | solution.py:405
  40.3 5.1 %shard_map.89 = (f32[16,8,1024]{2,1,0:T(8,128)}, f32[16,8,8,1024]{3,2,1,0:T(8,128)}, f32[8,1024]{1,0:T(8,128)}) custom-call(f32[16,8,1024]{2,1,0:T(8,128)} %vortex_hbm.3, f32[8,1024]{1,0:T(8,128)} %wind_hbm.1, s32[8,1024]{1,0:T(8,128)} %wet_hbm.1, f32[16,1024]{1,0:T(8,128)} %copy-done.2, f32[16,1024]{1,0:T(8,128)} %copy-done.3, ...), custom_call_target="tpu_custom_call" | custom-call | flops 16777216 | bytes 5242880 | tf_op jit(solution)/shard_map/pallas_call | solution.py:363
  45.4 5.2 %all-to-all-done.1.take_hbm = f32[128,1,256]{2,1,0:T(1,128)S(1)} async-done(((f32[128,1,256]{2,1,0:T(1,128)}), f32[128,1,256]{2,1,0:T(1,128)S(1)}, u32[]{:S(2)}, u32[]{:S(2)}) %all-to-all-start.1) | async-done | bytes 131104 | tf_op jit(solution)/shard_map/all_to_all | solution.py:405
  50.6 0.0 copy-start
  50.6 0.7 %copy-done = f32[128,1,256]{2,1,0:T(1,128)} copy-done((f32[128,1,256]{2,1,0:T(1,128)}, f32[128,1,256]{2,1,0:T(1,128)S(1)}, u32[]{:S(2)}) %copy-start) | copy-done | bytes 131096
  51.2 5.1 %shard_map.90 = (f32[16,8,1024]{2,1,0:T(8,128)}, f32[16,8,1024]{2,1,0:T(8,128)}) custom-call(s32[1]{0:T(128)} %bitcast.index_ref, f32[16]{0:T(128)} %radii_hbm.7, f32[128,1,256]{2,1,0:T(1,128)} %copy-done, f32[10,16,1024]{2,1,0:T(8,128)} %get-tuple-element.15.after_hbm.part_hbm, f32[160,160]{1,0:T(8,128)} %get-tuple-element.18.mixed_hbm, ...), custom_call_target="tpu_custom_call" | custom-call | flops 1006632960 | bytes 10485760 | tf_op jit(solution)/shard_map/pallas_call | solution.py:363
Async XLA Ops:
  5.0 21.7 %all-to-all-start = ((f32[128,1,256]{2,1,0:T(1,128)}), f32[128,1,256]{2,1,0:T(1,128)S(1)}, u32[]{:S(2)}, u32[]{:S(2)}) async-start(f32[128,1,256]{2,1,0:T(1,128)} %get-tuple-element.13), calls=%async_computation | async-start | bytes 262144 | tf_op jit(solution)/shard_map/all_to_all | solution.py:394
  16.5 7.8 %collective-permute-start = (f32[16,1024]{1,0:T(8,128)}, f32[16,1024]{1,0:T(8,128)S(1)}, u32[]{:S(2)}, u32[]{:S(2)}) collective-permute-start(f32[16,1024]{1,0:T(8,128)} %get-tuple-element.16), channel_id=1, source_target_pairs={{0,1},{1,2},{2,3},{3,4},{4,5},{5,6},{6,7},{7,8},{8,9},{9,10},{10,1... | collective-permute-start | bytes 196616 | tf_op jit(solution)/shard_map/ppermute | solution.py:395
  20.0 6.1 %collective-permute-start.1 = (f32[16,1024]{1,0:T(8,128)}, f32[16,1024]{1,0:T(8,128)S(1)}, u32[]{:S(2)}, u32[]{:S(2)}) collective-permute-start(f32[16,1024]{1,0:T(8,128)} %get-tuple-element.17), channel_id=1, source_target_pairs={{1,0},{2,1},{3,2},{4,3},{5,4},{6,5},{7,6},{8,7},{9,8},{10,9},{11,1... | collective-permute-start | bytes 196616 | tf_op jit(solution)/shard_map/ppermute | solution.py:396
  24.3 2.4 %copy-start.2 = (f32[16,1024]{1,0:T(8,128)}, f32[16,1024]{1,0:T(8,128)S(1)}, u32[]{:S(2)}) copy-start(f32[16,1024]{1,0:T(8,128)S(1)} %collective-permute-done.first_hbm.south_hbm) | copy-start | bytes 196612
  26.1 0.6 %copy-start.3 = (f32[16,1024]{1,0:T(8,128)}, f32[16,1024]{1,0:T(8,128)S(1)}, u32[]{:S(2)}) copy-start(f32[16,1024]{1,0:T(8,128)S(1)} %collective-permute-done.1.last_hbm.north_hbm) | copy-start | bytes 196612
  26.7 0.7 %copy-start.1 = (f32[128,1,256]{2,1,0:T(1,128)}, f32[128,1,256]{2,1,0:T(1,128)S(1)}, u32[]{:S(2)}) copy-start(f32[128,1,256]{2,1,0:T(1,128)S(1)} %all-to-all-done.take_hbm) | copy-start | bytes 393220
  29.2 21.3 %all-to-all-start.1 = ((f32[128,1,256]{2,1,0:T(1,128)}), f32[128,1,256]{2,1,0:T(1,128)S(1)}, u32[]{:S(2)}, u32[]{:S(2)}) async-start(f32[128,1,256]{2,1,0:T(1,128)} %shard_map.88.after_hbm), calls=%async_computation.1 | async-start | bytes 262144 | tf_op jit(solution)/shard_map/all_to_all | solution.py:405
  50.6 0.7 %copy-start = (f32[128,1,256]{2,1,0:T(1,128)}, f32[128,1,256]{2,1,0:T(1,128)S(1)}, u32[]{:S(2)}) copy-start(f32[128,1,256]{2,1,0:T(1,128)S(1)} %all-to-all-done.1.take_hbm) | copy-start | bytes 393220

commit v2 on v1

--- a/solution.py
+++ b/solution.py
@@ -23,6 +23,7 @@
 AXES = ("group", "tile")
 HIGHEST = lax.Precision.HIGHEST
 SMEM = pl.BlockSpec(memory_space=pltpu.SMEM)
+VMEM = pl.BlockSpec(memory_space=pltpu.VMEM)
 ANY = pl.BlockSpec(memory_space=pl.ANY)
 DMA = pltpu.SemaphoreType.DMA
 f32, bf16, i32 = jnp.float32, jnp.bfloat16, jnp.int32
@@ -104,9 +105,9 @@
 
 def forward_kernel(
     vortex_hbm, mix_hbm, radii_hbm, table_hbm,
-    send_hbm, force_hbm, first_hbm, last_hbm, high_hbm, low_hbm,
+    send_hbm, force_hbm, high_hbm, low_hbm,
     vortex_ref, mix_ref, radii_ref, table_ref,
-    send_ref, force_ref, first_ref, last_ref, high_ref, low_ref, sems,
+    send_ref, force_ref, high_ref, low_ref, sems,
 ):
     copies = fetch(
         [(mix_hbm, mix_ref), (radii_hbm, radii_ref), (vortex_hbm, vortex_ref), (table_hbm, table_ref)], sems
@@ -119,9 +120,11 @@
     mix = jnp.concatenate([wide] * ROWS, 0)
     mix = jnp.where(iota((rows, rows), 0) // NL == iota((rows, rows), 1) % ROWS, mix, 0.0)
     wait(copies[2:3])
-    first_ref[...] = vortex_ref[:, 0]
-    last_ref[...] = vortex_ref[:, ROWS - 1]
-    written = fetch([(first_ref, first_hbm), (last_ref, last_hbm)], sems, 4)
+    written = []
+    for c in range(N // LANES):
+        part = slice(c * LANES, (c + 1) * LANES)
+        send_ref[c * NL : (c + 1) * NL, 0, 2 * LANES : 3 * LANES] = vortex_ref[:, ROWS - 1, part]
+        send_ref[c * NL : (c + 1) * NL, 0, 3 * LANES :] = vortex_ref[:, 0, part]
     modal = split_dot(halves(mix), halves(vortex_ref[...].reshape(rows, N)))
     split = halves(modal)
     wait(copies[3:])
@@ -133,7 +136,7 @@
             high, low = halves(block)
             high_ref[n, 32 * a : 32 * a + 32] = high
             low_ref[n, 32 * a : 32 * a + 32] = low
-        written += fetch([(high_ref.at[n], high_hbm.at[n]), (low_ref.at[n], low_hbm.at[n])], sems, 6 + 3 * n)
+        written += fetch([(high_ref.at[n], high_hbm.at[n]), (low_ref.at[n], low_hbm.at[n])], sems, 4 + 3 * n)
         spectrum = split_dot(split, (high_ref[n], low_ref[n]))
         right = jnp.zeros((NL, STEP), jnp.float32)
         left = jnp.zeros((NL, STEP), jnp.float32)
@@ -148,10 +151,10 @@
             dest = n * (STEP // LANES) + c
             part = slice(c * LANES, (c + 1) * LANES)
             send_ref[dest * NL : (dest + 1) * NL, 0, :LANES] = right[:, part]
-            send_ref[dest * NL : (dest + 1) * NL, 0, LANES:] = left[:, part]
+            send_ref[dest * NL : (dest + 1) * NL, 0, LANES : 2 * LANES] = left[:, part]
         dests = pl.ds(n * (STEP // LANES) * NL, STEP // LANES * NL)
-        written += fetch([(send_ref.at[dests], send_hbm.at[dests])], sems, 8 + 3 * n)
-    written += fetch([(force_ref, force_hbm)], sems, 6 + 3 * PIECES)
+        written += fetch([(send_ref.at[dests], send_hbm.at[dests])], sems, 6 + 3 * n)
+    written += fetch([(force_ref, force_hbm)], sems, 4 + 3 * PIECES)
     wait(written)
 
 
@@ -163,11 +166,10 @@
 
 
 def scan_kernel(
-    index_ref, radii_hbm, take_hbm, after_hbm, first_hbm, last_hbm, give_hbm, radii_ref, take_ref, give_ref, sems
+    index_ref, take_ref, radii_hbm, after_hbm, give_hbm, radii_ref, give_ref, sems
 ):
-    del after_hbm, first_hbm, last_hbm
-    copies = fetch([(radii_hbm, radii_ref), (take_hbm, take_ref)], sems)
-    copies[0].wait()
+    del after_hbm
+    wait(fetch([(radii_hbm, radii_ref)], sems))
     me = index_ref[0]
     rho, _ = decay_of(eigen_values(me // NL * LANES, LANES) + radii_ref[me % NL])
     rho2 = rho * rho
@@ -182,9 +184,8 @@
         odd = (place >> bit) % 2 == 1
         power = power * jnp.where(odd, rate, 1.0)
         reverse = reverse * jnp.where(odd, 1.0, rate)
-    copies[1].wait()
     right = take_ref[:, 0, :LANES]
-    left = take_ref[:, 0, LANES:]
+    left = take_ref[:, 0, LANES : 2 * LANES]
     for bit, rate in enumerate(rates[:-1]):
         right = right + rate * shift_rows(right, 1 << bit)
         left = left + rate * shift_rows(left, -1 << bit)
@@ -195,7 +196,9 @@
     alpha = -(below - far * above) * scale
     beta = -(above - far * below) * scale
     give_ref[:, 0, :LANES] = shift_rows(right, 1) + alpha * power
-    give_ref[:, 0, LANES:] = shift_rows(left, -1) + beta * reverse
+    give_ref[:, 0, LANES : 2 * LANES] = shift_rows(left, -1) + beta * reverse
+    give_ref[:, 0, 2 * LANES : 3 * LANES] = shift_rows(take_ref[:, 0, 2 * LANES : 3 * LANES], 1)
+    give_ref[:, 0, 3 * LANES :] = shift_rows(take_ref[:, 0, 3 * LANES :], -1)
     wait(fetch([(give_ref, give_hbm)], sems))
 
 
@@ -244,17 +247,12 @@
 
 
 def weight_kernel(
-    vortex_hbm, wind_hbm, wet_hbm, south_hbm, north_hbm, after_hbm, base_hbm, coef_hbm, drag_hbm,
-    vortex_ref, wind_ref, wet_ref, south_ref, north_ref, base_ref, coef_ref, drag_ref, sems,
+    vortex_hbm, wind_hbm, wet_hbm, after_hbm, coef_hbm, vortex_ref, wind_ref, wet_ref, coef_ref, sems
 ):
     del after_hbm
     wait(
         fetch(
-            [
-                (wet_hbm, wet_ref), (wind_hbm, wind_ref), (south_hbm, south_ref), (north_hbm, north_ref),
-                (vortex_hbm, vortex_ref),
-            ],
-            sems,
+            [(wet_hbm, wet_ref), (wind_hbm, wind_ref), (vortex_hbm, vortex_ref)], sems
         )
     )
     keep = time_step * wet_ref[...].astype(jnp.float32)
@@ -262,8 +260,8 @@
     written = []
     for layer in range(NL):
         mid = vortex_ref[layer]
-        north = roll_sub(mid, north_ref[layer : layer + 1], -1)
-        south = roll_sub(mid, south_ref[layer : layer + 1], 1)
+        north = roll_sub(mid, 0.0, -1)
+        south = roll_sub(mid, 0.0, 1)
         east = roll_lanes(mid, -1)
         west = roll_lanes(mid, 1)
         north_east = roll_lanes(north, -1)
@@ -282,7 +280,8 @@
             c_west = c_west - drag
             c_north = c_north - drag
             c_south = c_south - drag
-            drag_ref[...] = 4.0 * drag
+            coef_ref[NL, 0] = 4.0 * drag
+            coef_ref[NL, 1] = twelfth
         coef_ref[layer, 0] = c_north
         coef_ref[layer, 1] = c_south
         coef_ref[layer, 2] = roll_lanes(c_east, 1)
@@ -291,35 +290,29 @@
         coef_ref[layer, 5] = roll_lanes(c_west, -1)
         coef_ref[layer, 6] = roll_lanes(twelfth * (north - west), -1)
         coef_ref[layer, 7] = roll_lanes(-twelfth * (south - west), -1)
-        base_ref[layer] = mid + keep * wind_ref[...] if layer == 0 else mid
+        coef_ref[layer, 8] = mid + keep * wind_ref[...] if layer == 0 else mid
         if layer % 4 == 3:
-            some = pl.ds(layer - 3, 4)
-            written += fetch([(coef_ref.at[some], coef_hbm.at[some])], sems, 5 + layer // 4)
-    wait(written + fetch([(base_ref, base_hbm), (drag_ref, drag_hbm)], sems, 9))
+            some = pl.ds(layer - 3, 4 if layer < NL - 1 else 5)
+            written += fetch([(coef_ref.at[some], coef_hbm.at[some])], sems, 3 + layer // 4)
+    wait(written)
 
 
 def backward_kernel(
-    index_ref, radii_hbm, take_hbm, part_hbm, mixed_hbm, high_hbm, low_hbm, base_hbm, coef_hbm, drag_hbm,
-    vortex_hbm, stream_hbm,
-    radii_ref, take_ref, part_ref, mixed_ref, high_ref, low_ref, base_ref, coef_ref, drag_ref,
-    psi_ref, wave_ref, vortex_ref, stream_ref, sems,
+    index_ref, take_ref, part_ref, mixed_ref, radii_hbm, high_hbm, low_hbm, coef_hbm, vortex_hbm, stream_hbm,
+    radii_ref, high_ref, low_ref, coef_ref, psi_ref, south_ref, north_ref, wave_ref, vortex_ref, stream_ref, sems,
 ):
     copies = fetch(
-        [
-            (radii_hbm, radii_ref), (take_hbm, take_ref), (part_hbm, part_ref), (mixed_hbm, mixed_ref),
-            (high_hbm, high_ref), (low_hbm, low_ref), (coef_hbm, coef_ref), (base_hbm, base_ref),
-            (drag_hbm, drag_ref),
-        ],
-        sems,
+        [(radii_hbm, radii_ref), (high_hbm, high_ref), (low_hbm, low_ref), (coef_hbm, coef_ref)], sems
     )
     out = len(copies)
     copies[0].wait()
     rho, _ = mode_decay(radii_ref)
-    wait(copies[1:3])
     for c in range(N // LANES):
         cols = slice(c * LANES, (c + 1) * LANES)
         up = take_ref[c * NL : (c + 1) * NL, 0, :LANES]
-        down = take_ref[c * NL : (c + 1) * NL, 0, LANES:]
+        down = take_ref[c * NL : (c + 1) * NL, 0, LANES : 2 * LANES]
+        south_ref[:, cols] = take_ref[c * NL : (c + 1) * NL, 0, 2 * LANES : 3 * LANES]
+        north_ref[:, cols] = take_ref[c * NL : (c + 1) * NL, 0, 3 * LANES :]
         near = rho[:, cols]
         ups, downs = [up], [down]
         for _ in range(ROWS + 1):
@@ -327,9 +320,8 @@
             downs.append(downs[-1] * near)
         for i in range(TALL):
             psi_ref[i * NL : (i + 1) * NL, cols] = part_ref[i, :, cols] + ups[i] + downs[ROWS + 1 - i]
-    wait(copies[3:4])
     split = halves(split_dot(halves(mixed_ref[...]), halves(psi_ref[...])))
-    wait(copies[4:6])
+    wait(copies[1:3])
     for n in range(PIECES):
         wave_ref[:, n * STEP : (n + 1) * STEP] = split_dot(split, (high_ref[n], low_ref[n]))
     inside_low = jnp.where(index_ref[0] > 0, 1.0, 0.0)
@@ -338,14 +330,25 @@
     for layer in range(NL):
         stream_ref[layer] = wave_ref[layer * ROWS : (layer + 1) * ROWS]
     written = fetch([(stream_ref, stream_hbm)], sems, out)
-    wait(copies[6:])
+    wait(copies[3:])
+    twelfth = coef_ref[NL, 1]
+    for y, edge_ref, beyond, sign in (
+        (0, south_ref, inside_low * wave_ref[body : body + NL], 1.0),
+        (ROWS - 1, north_ref, inside_high * wave_ref[body + NL :], -1.0),
+    ):
+        here = stream_ref[:, y]
+        edge = edge_ref[...]
+        east, west = roll_lanes(edge, -1), roll_lanes(edge, 1)
+        more = roll_lanes(here, -1) * (edge + east) - roll_lanes(here, 1) * (edge + west)
+        more += edge * (roll_lanes(beyond, -1) - roll_lanes(beyond, 1)) - beyond * (east - west)
+        coef_ref[:NL, 8, y] += sign * twelfth[y : y + 1] * more
     for layer in range(NL):
         mid = wave_ref[layer * ROWS : (layer + 1) * ROWS]
         north = roll_sub(mid, inside_high * wave_ref[body + NL + layer : body + NL + layer + 1], -1)
         south = roll_sub(mid, inside_low * wave_ref[body + layer : body + layer + 1], 1)
-        total = base_ref[layer] + coef_ref[layer, 0] * north + coef_ref[layer, 1] * south
+        total = coef_ref[layer, 8] + coef_ref[layer, 0] * north + coef_ref[layer, 1] * south
         if layer == NL - 1:
-            total = total + drag_ref[...] * mid
+            total = total + coef_ref[NL, 0] * mid
         from_east = coef_ref[layer, 2] * mid + coef_ref[layer, 3] * north + coef_ref[layer, 4] * south
         from_west = coef_ref[layer, 5] * mid + coef_ref[layer, 6] * north + coef_ref[layer, 7] * south
         vortex_ref[layer] = total + pltpu.roll(from_east, N - 1, 1) + pltpu.roll(from_west, 1, 1)
@@ -355,20 +358,19 @@
     wait(written)
 
 
-def call(kernel, outs, args, scratch, flops, nbytes, index=None, limit=60 * 1024 * 1024):
+def call(kernel, outs, args, scratch, flops, nbytes, scalars=(), near=(), limit=60 * 1024 * 1024):
     def room(kind):
         return pltpu.VMEM(*kind) if isinstance(kind, tuple) else kind
 
-    lead = [] if index is None else [index]
     return pl.pallas_call(
         kernel,
         out_shape=[jax.ShapeDtypeStruct(s, d) for s, d in outs],
-        in_specs=[SMEM] * len(lead) + [ANY] * len(args),
+        in_specs=[SMEM] * len(scalars) + [VMEM] * len(near) + [ANY] * len(args),
         out_specs=[ANY] * len(outs),
         scratch_shapes=[room(kind) for kind in scratch],
         compiler_params=pltpu.CompilerParams(vmem_limit_bytes=limit),
         cost_estimate=pl.CostEstimate(flops=flops, bytes_accessed=nbytes, transcendentals=0),
-    )(*lead, *args)
+    )(*scalars, *near, *args)
 
 
 def body(vorticity, layer_to_mode, mode_to_layer, inverse_radii, wind_curl, wet_mask):
@@ -377,43 +379,41 @@
     edge = ((NL, N), f32)
     mixing = ((NL, NL), f32)
     sines = ((PIECES, N, STEP), bf16)
-    packet = ((BLOCKS, 1, 2 * LANES), f32)
+    packet = ((BLOCKS, 1, 4 * LANES), f32)
     rows = ((ROWS, NL, N), f32)
     rates = pltpu.SMEM((NL,), f32)
     parts = [((TALL, NL, N), f32), ((NL * TALL, NL * TALL), f32)]
-    weights = [field, ((NL, 8, ROWS, N), f32), plane]
+    weights = ((NL + 1, 9, ROWS, N), f32)
     wave = ((NL * TALL, N), f32)
 
     index = (lax.axis_index("group") * lax.axis_size("tile") + lax.axis_index("tile")).astype(i32).reshape(1)
-    outs = [packet, rows, edge, edge, sines, sines]
-    send, force, first, last, high, low = call(
+    outs = [packet, rows, sines, sines]
+    send, force, high, low = call(
         forward_kernel, outs, (vorticity, layer_to_mode, inverse_radii, jnp.asarray(host_table())),
-        [field, mixing, rates, ((4, 32, N), f32), *outs, DMA((7 + 3 * PIECES,))],
+        [field, mixing, rates, ((4, 32, N), f32), *outs, DMA((5 + 3 * PIECES,))],
         6 * 128 * N * N, 6 << 20,
     )
     take = lax.all_to_all(send, AXES, split_axis=0, concat_axis=0, tiled=True)
-    south = lax.ppermute(last, AXES, [(i, i + 1) for i in range(BLOCKS - 1)])
-    north = lax.ppermute(first, AXES, [(i + 1, i) for i in range(BLOCKS - 1)])
     part, mixed = call(
         part_kernel, parts, (force, inverse_radii, mode_to_layer), [rows, rates, mixing, *parts, DMA((5,))],
         1 << 24, 1 << 20,
     )
     (give,) = call(
-        scan_kernel, [packet], (inverse_radii, take, part, south, north), [rates, packet, packet, DMA((2,))],
-        1 << 22, 1 << 18, index,
+        scan_kernel, [packet], (inverse_radii, part), [rates, packet, DMA((1,))],
+        1 << 22, 1 << 18, [index], [take], limit=54500 << 10,
     )
     amplitude = lax.all_to_all(give, AXES, split_axis=0, concat_axis=0, tiled=True)
-    base, coef, drag = call(
-        weight_kernel, weights, (vorticity, wind_curl, wet_mask, south, north, give),
-        [field, plane, ((ROWS, N), i32), edge, edge, *weights, DMA((11,))],
+    (coef,) = call(
+        weight_kernel, [weights], (vorticity, wind_curl, wet_mask, give),
+        [field, plane, ((ROWS, N), i32), weights, DMA((7,))],
         1 << 24, 5 << 20,
     )
     return tuple(
         call(
             backward_kernel, [field, field],
-            (inverse_radii, amplitude, part, mixed, high, low, base, coef, drag),
-            [rates, packet, *parts, sines, sines, *weights, wave, wave, field, field, DMA((14,))],
-            6 * 160 * N * N, 10 << 20, index,
+            (inverse_radii, high, low, coef),
+            [rates, sines, sines, weights, wave, edge, edge, wave, field, field, DMA((9,))],
+            6 * 160 * N * N, 10 << 20, [index], [amplitude, part, mixed], limit=53500 << 10,
         )
     )
 

time: 56.6 us -> 50.9 us (0.90)
  starting transfers between devices: 28.1 us -> 15.3 us
  waiting for transfers between devices: 7.56 us -> 15.8 us
  local copies, waits for them, and re-layouts: 1.31 us -> 0.01 us
    all_to_all x1, waiting for transfers between devices: 0.58 us -> 9.19 us  [body(): take = lax.all_to_all(send, AXES, split_axis=0, concat_axis=0, tiled=True)]
    all_to_all x1, starting transfers between devices: 11.1 us -> 3.82 us  [body(): lax.all_to_all(give, AXES, split_axis=0, concat_axis=0, tiled=True)]
    ppermute x2 -> x0, starting transfers between devices: 5.46 us -> none  [the longest x1 3.54 us: body(): south = lax.ppermute(last, AXES, [(i, i + 1) for i in range(BLOCKS - 1)])]
    ppermute x2 -> x0, waiting for transfers between devices: 1.81 us -> none  [the longest x1 1.81 us: body(): north = lax.ppermute(first, AXES, [(i + 1, i) for i in range(BLOCKS - 1)])]
    all_to_all x1, waiting for transfers between devices: 5.16 us -> 6.65 us  [body(): lax.all_to_all(give, AXES, split_axis=0, concat_axis=0, tiled=True)]
    unnamed x8 -> x6, local copies, waits for them, and re-layouts: 1.31 us -> 0.01 us
  transfers between devices with their start and end apart: 4 -> 2, of which waited for: 3 -> 2; matrix products, arithmetic and copies ran while one was open for 0% -> 0% of each run, Pallas kernels for 13% -> 14%
where the time goes in v2:
time: 50.9 us; the launch traced here: 50.6 us
  Pallas kernels  18.7 us (37%)
  waiting for transfers between devices  15.8 us (31%)
  starting transfers between devices  15.3 us (30%)
  between operations  0.71 us (1%)
    pallas_call x5, Pallas kernels, call(): pl.pallas_call(kernel, out_shape=[jax.ShapeDtypeStruct(s, d) for s, d in...  18.7 us
    all_to_all x1, starting transfers between devices, body(): take = lax.all_to_all(send, AXES, split_axis=0, concat_axis=0, tiled=True)  11.5 us
    all_to_all x1, waiting for transfers between devices, body(): take = lax.all_to_all(send, AXES, split_axis=0, concat_axis=0, tiled=True)  9.19 us
    all_to_all x1, waiting for transfers between devices, body(): lax.all_to_all(give, AXES, split_axis=0, concat_axis=0, tiled=True)  6.65 us
    all_to_all x1, starting transfers between devices, body(): lax.all_to_all(give, AXES, split_axis=0, concat_axis=0, tiled=True)  3.82 us
  transfers between devices with their start and end apart: 2, of which 2 were waited for; matrix products, arithmetic and copies ran while one was open for 0% of the time, Pallas kernels for 14%

profile of v2, /device:TPU:1, one launch (start us, length us, event | category | flops | bytes accessed | tf_op | source)
XLA Modules:
  0.0 50.6 jit_solution(5743547248852564024)
XLA Ops:
  0.6 0.0 copy-start.2
  0.6 4.4 %shard_map.86 = (f32[128,1,512]{2,1,0:T(1,128)}, f32[8,16,1024]{2,1,0:T(8,128)}, bf16[4,1024,256]{2,1,0:T(8,128)(2,1)}, bf16[4,1024,256]{2,1,0:T(8,128)(2,1)}) custom-call(f32[16,8,1024]{2,1,0:T(8,128)} %vortex_hbm.3, f32[16,16]{1,0:T(8,128)} %mix_hbm.2, f32[16]{0:T(128)} %radii_hbm.7, f32[4,32,1024]{2,1,0:T(8,128)} %constant.13.clone.table_hbm), custom_call_target="tpu_custom_call" | custom-call | flops 805306368 | bytes 6291456 | tf_op jit(solution)/shard_map/pallas_call | solution.py:365
  5.1 11.5 %all-to-all-start = ((f32[128,1,512]{2,1,0:T(1,128)}), f32[128,1,512]{2,1,0:T(1,128)S(1)}, u32[]{:S(2)}, u32[]{:S(2)}) async-start(f32[128,1,512]{2,1,0:T(1,128)} %get-tuple-element.8), calls=%async_computation | async-start | bytes 524288 | tf_op jit(solution)/shard_map/all_to_all | solution.py:396
  16.6 2.3 %shard_map.87 = (f32[10,16,1024]{2,1,0:T(8,128)}, f32[160,160]{1,0:T(8,128)}) custom-call(f32[8,16,1024]{2,1,0:T(8,128)} %get-tuple-element.9.force_hbm, f32[16]{0:T(128)} %radii_hbm.7, f32[16,16]{1,0:T(8,128)} %mix_hbm.3), custom_call_target="tpu_custom_call" | custom-call | flops 16777216 | bytes 1048576 | tf_op jit(solution)/shard_map/pallas_call | solution.py:365
  18.8 9.2 %all-to-all-done.take_ref = f32[128,1,512]{2,1,0:T(1,128)S(1)} async-done(((f32[128,1,512]{2,1,0:T(1,128)}), f32[128,1,512]{2,1,0:T(1,128)S(1)}, u32[]{:S(2)}, u32[]{:S(2)}) %all-to-all-start) | async-done | bytes 262176 | tf_op jit(solution)/shard_map/all_to_all | solution.py:396
  28.0 0.0 copy-done.2
  28.0 1.9 %shard_map.88.after_hbm = f32[128,1,512]{2,1,0:T(1,128)} custom-call(s32[1]{0:T(128)} %bitcast.index_ref, f32[128,1,512]{2,1,0:T(1,128)S(1)} %all-to-all-done.take_ref, f32[16]{0:T(128)S(1)} %copy-done.2, f32[10,16,1024]{2,1,0:T(8,128)} %get-tuple-element.10.after_hbm.part_ref), custom_call_target="tpu_custom_call" | custom-call | flops 4194304 | bytes 262144 | tf_op jit(solution)/shard_map/pallas_call | solution.py:365
  30.0 3.8 %all-to-all-start.1 = ((f32[128,1,512]{2,1,0:T(1,128)}), f32[128,1,512]{2,1,0:T(1,128)S(1)}, u32[]{:S(2)}, u32[]{:S(2)}) async-start(f32[128,1,512]{2,1,0:T(1,128)} %shard_map.88.after_hbm), calls=%async_computation.1 | async-start | bytes 524288 | tf_op jit(solution)/shard_map/all_to_all | solution.py:405
  33.8 0.0 copy-start
  33.8 0.0 copy-start.1
  33.8 4.9 %shard_map.89.coef_hbm = f32[17,9,8,1024]{3,2,1,0:T(8,128)} custom-call(f32[16,8,1024]{2,1,0:T(8,128)} %vortex_hbm.3, f32[8,1024]{1,0:T(8,128)} %wind_hbm.1, s32[8,1024]{1,0:T(8,128)} %wet_hbm.1, f32[128,1,512]{2,1,0:T(1,128)} %shard_map.88.after_hbm), custom_call_target="tpu_custom_call" | custom-call | flops 16777216 | bytes 5242880 | tf_op jit(solution)/shard_map/pallas_call | solution.py:365
  38.8 6.7 %all-to-all-done.1.take_ref = f32[128,1,512]{2,1,0:T(1,128)S(1)} async-done(((f32[128,1,512]{2,1,0:T(1,128)}), f32[128,1,512]{2,1,0:T(1,128)S(1)}, u32[]{:S(2)}, u32[]{:S(2)}) %all-to-all-start.1) | async-done | bytes 262176 | tf_op jit(solution)/shard_map/all_to_all | solution.py:405
  45.4 0.0 copy-done
  45.4 0.0 copy-done.1
  45.4 5.2 %shard_map.90 = (f32[16,8,1024]{2,1,0:T(8,128)}, f32[16,8,1024]{2,1,0:T(8,128)}) custom-call(s32[1]{0:T(128)} %bitcast.index_ref, f32[128,1,512]{2,1,0:T(1,128)S(1)} %all-to-all-done.1.take_ref, f32[10,16,1024]{2,1,0:T(8,128)S(1)} %copy-done, f32[160,160]{1,0:T(8,128)S(1)} %copy-done.1, f32[16]{0:T(128)S(1)} %copy-done.2, ...), custom_call_target="tpu_custom_call" | custom-call | flops 1006632960 | bytes 10485760 | tf_op jit(solution)/shard_map/pallas_call | solution.py:365
Async XLA Ops:
  0.6 27.4 %copy-start.2 = (f32[16]{0:T(128)S(1)}, f32[16]{0:T(128)}, u32[]{:S(2)}) copy-start(f32[16]{0:T(128)} %radii_hbm.7) | copy-start | bytes 196
  5.1 23.0 %all-to-all-start = ((f32[128,1,512]{2,1,0:T(1,128)}), f32[128,1,512]{2,1,0:T(1,128)S(1)}, u32[]{:S(2)}, u32[]{:S(2)}) async-start(f32[128,1,512]{2,1,0:T(1,128)} %get-tuple-element.8), calls=%async_computation | async-start | bytes 524288 | tf_op jit(solution)/shard_map/all_to_all | solution.py:396
  30.0 15.4 %all-to-all-start.1 = ((f32[128,1,512]{2,1,0:T(1,128)}), f32[128,1,512]{2,1,0:T(1,128)S(1)}, u32[]{:S(2)}, u32[]{:S(2)}) async-start(f32[128,1,512]{2,1,0:T(1,128)} %shard_map.88.after_hbm), calls=%async_computation.1 | async-start | bytes 524288 | tf_op jit(solution)/shard_map/all_to_all | solution.py:405
  33.8 11.6 %copy-start = (f32[10,16,1024]{2,1,0:T(8,128)S(1)}, f32[10,16,1024]{2,1,0:T(8,128)}, u32[]{:S(2)}) copy-start(f32[10,16,1024]{2,1,0:T(8,128)} %get-tuple-element.10.after_hbm.part_ref) | copy-start | bytes 1966084
  33.8 11.6 %copy-start.1 = (f32[160,160]{1,0:T(8,128)S(1)}, f32[160,160]{1,0:T(8,128)}, u32[]{:S(2)}) copy-start(f32[160,160]{1,0:T(8,128)} %get-tuple-element.11.mixed_ref) | copy-start | bytes 307204

commit v3 on v2

--- a/solution.py
+++ b/solution.py
@@ -18,6 +18,7 @@
 TALL = ROWS + 2
 BLOCKS = 128
 LANES = 128
+HALF = N // 2
 STEP = 256
 PIECES = N // STEP
 AXES = ("group", "tile")
@@ -31,21 +32,20 @@
 
 def host_table():
     k = np.arange(1, N + 1)
-    turn = 2 * (N + 1)
-    angle_a = np.pi * ((32 * np.arange(32)[:, None] * k[None, :]) % turn) / (N + 1)
-    angle_b = np.pi * ((np.arange(1, 33)[:, None] * k[None, :]) % turn) / (N + 1)
-    scale = math.sqrt(2.0 / (N + 1))
-    table = [np.sin(angle_a), np.cos(angle_a), scale * np.sin(angle_b), scale * np.cos(angle_b)]
-    return np.stack(table).astype(np.float32)
+    sine = math.sqrt(2.0 / (N + 1)) * np.sin(np.pi * ((k[:, None] * k[None, :]) % (2 * (N + 1))) / (N + 1))
+    table = np.stack([sine[:HALF, 0::2], sine[:HALF, 1::2]])
+    high = table.astype(jnp.bfloat16)
+    low = (table - high.astype(np.float64)).astype(jnp.bfloat16)
+    return np.stack([high, low], 1)
 
 
 def iota(shape, dim):
     return lax.broadcasted_iota(jnp.int32, shape, dim)
 
 
-def dot(left, right, precision=None):
+def dot(left, right, precision=None, across=0):
     return lax.dot_general(
-        left, right, (((1,), (0,)), ((), ())), precision=precision, preferred_element_type=jnp.float32
+        left, right, (((1,), (across,)), ((), ())), precision=precision, preferred_element_type=jnp.float32
     )
 
 
@@ -55,10 +55,18 @@
     return high, low
 
 
-def split_dot(left, right):
+def split_dot(left, right, across=0):
     count = left[0].shape[0]
-    both = dot(jnp.concatenate(left, 0), right[0])
-    return both[:count] + both[count:] + dot(left[0], right[1])
+    both = dot(jnp.concatenate(left, 0), right[0], None, across)
+    return both[:count] + both[count:] + dot(left[0], right[1], None, across)
+
+
+def mirrored(value):
+    flip = (iota((STEP, STEP), 0) + iota((STEP, STEP), 1) == STEP - 1).astype(jnp.bfloat16)
+    count, width = value.shape
+    parts = jnp.concatenate(halves(value), 0)
+    blocks = [dot(parts[:, i : i + STEP], flip) for i in range(0, width, STEP)]
+    return jnp.concatenate([block[:count] + block[count:] for block in reversed(blocks)], 1)
 
 
 def fetch(pairs, sems, first=0):
@@ -74,7 +82,8 @@
 
 
 def eigen_values(first, width):
-    wave = (iota((1, width), 1) + (first + 1)).astype(jnp.float32)
+    column = iota((1, width), 1) + first
+    wave = jnp.where(column < HALF, 2 * column + 1, 2 * column + 2 - N).astype(jnp.float32)
     angle = wave * (math.pi / (2 * (N + 1)))
     square = angle * angle
     series = jnp.full_like(square, 1.0 / math.factorial(15))
@@ -105,12 +114,15 @@
 
 def forward_kernel(
     vortex_hbm, mix_hbm, radii_hbm, table_hbm,
-    send_hbm, force_hbm, high_hbm, low_hbm,
-    vortex_ref, mix_ref, radii_ref, table_ref,
-    send_ref, force_ref, high_ref, low_ref, sems,
+    send_hbm, force_hbm,
+    vortex_ref, mix_ref, radii_ref, table_ref, send_ref, force_ref, sems,
 ):
     copies = fetch(
-        [(mix_hbm, mix_ref), (radii_hbm, radii_ref), (vortex_hbm, vortex_ref), (table_hbm, table_ref)], sems
+        [
+            (mix_hbm, mix_ref), (radii_hbm, radii_ref), (vortex_hbm, vortex_ref),
+            (table_hbm.at[0], table_ref.at[0]), (table_hbm.at[1], table_ref.at[1]),
+        ],
+        sems,
     )
     rows = NL * ROWS
     spread = (iota((NL, rows), 1) // ROWS == iota((NL, rows), 0)).astype(jnp.float32)
@@ -126,18 +138,15 @@
         send_ref[c * NL : (c + 1) * NL, 0, 2 * LANES : 3 * LANES] = vortex_ref[:, ROWS - 1, part]
         send_ref[c * NL : (c + 1) * NL, 0, 3 * LANES :] = vortex_ref[:, 0, part]
     modal = split_dot(halves(mix), halves(vortex_ref[...].reshape(rows, N)))
-    split = halves(modal)
-    wait(copies[3:])
+    mirror = mirrored(modal[:, HALF:])
+    folded = [halves(modal[:, :HALF] + mirror), halves(modal[:, :HALF] - mirror)]
     for n in range(PIECES):
         cols = slice(n * STEP, (n + 1) * STEP)
-        for a in range(32):
-            block = table_ref[0, a : a + 1, cols] * table_ref[3, :, cols]
-            block += table_ref[1, a : a + 1, cols] * table_ref[2, :, cols]
-            high, low = halves(block)
-            high_ref[n, 32 * a : 32 * a + 32] = high
-            low_ref[n, 32 * a : 32 * a + 32] = low
-        written += fetch([(high_ref.at[n], high_hbm.at[n]), (low_ref.at[n], low_hbm.at[n])], sems, 4 + 3 * n)
-        spectrum = split_dot(split, (high_ref[n], low_ref[n]))
+        odd, start = divmod(n * STEP, HALF)
+        if start == 0:
+            copies[3 + odd].wait()
+        some = slice(start, start + STEP)
+        spectrum = split_dot(folded[odd], (table_ref[odd, 0, :, some], table_ref[odd, 1, :, some]))
         right = jnp.zeros((NL, STEP), jnp.float32)
         left = jnp.zeros((NL, STEP), jnp.float32)
         force = []
@@ -153,8 +162,8 @@
             send_ref[dest * NL : (dest + 1) * NL, 0, :LANES] = right[:, part]
             send_ref[dest * NL : (dest + 1) * NL, 0, LANES : 2 * LANES] = left[:, part]
         dests = pl.ds(n * (STEP // LANES) * NL, STEP // LANES * NL)
-        written += fetch([(send_ref.at[dests], send_hbm.at[dests])], sems, 6 + 3 * n)
-    written += fetch([(force_ref, force_hbm)], sems, 4 + 3 * PIECES)
+        written += fetch([(send_ref.at[dests], send_hbm.at[dests])], sems, 5 + n)
+    written += fetch([(force_ref, force_hbm)], sems, 5 + PIECES)
     wait(written)
 
 
@@ -165,25 +174,9 @@
     return jnp.concatenate([value[-step:], blank], 0)
 
 
-def scan_kernel(
-    index_ref, take_ref, radii_hbm, after_hbm, give_hbm, radii_ref, give_ref, sems
-):
-    del after_hbm
-    wait(fetch([(radii_hbm, radii_ref)], sems))
-    me = index_ref[0]
-    rho, _ = decay_of(eigen_values(me // NL * LANES, LANES) + radii_ref[me % NL])
-    rho2 = rho * rho
-    rho4 = rho2 * rho2
-    place = iota((BLOCKS, LANES), 0)
-    rates = [rho4 * rho4]
-    while 2 ** len(rates) <= BLOCKS:
-        rates.append(rates[-1] * rates[-1])
-    power = jnp.ones((BLOCKS, LANES), jnp.float32)
-    reverse = power
-    for bit, rate in enumerate(rates[:-1]):
-        odd = (place >> bit) % 2 == 1
-        power = power * jnp.where(odd, rate, 1.0)
-        reverse = reverse * jnp.where(odd, 1.0, rate)
+def scan_kernel(take_ref, ends_ref, give_hbm, give_ref, sems):
+    rates = [ends_ref[2 * BLOCKS + bit : 2 * BLOCKS + bit + 1] for bit in range(8)]
+    rho = ends_ref[2 * BLOCKS + 8 : 2 * BLOCKS + 9]
     right = take_ref[:, 0, :LANES]
     left = take_ref[:, 0, LANES : 2 * LANES]
     for bit, rate in enumerate(rates[:-1]):
@@ -195,18 +188,37 @@
     scale = 1.0 / (1.0 - far * far)
     alpha = -(below - far * above) * scale
     beta = -(above - far * below) * scale
-    give_ref[:, 0, :LANES] = shift_rows(right, 1) + alpha * power
-    give_ref[:, 0, LANES : 2 * LANES] = shift_rows(left, -1) + beta * reverse
+    give_ref[:, 0, :LANES] = shift_rows(right, 1) + alpha * ends_ref[:BLOCKS]
+    give_ref[:, 0, LANES : 2 * LANES] = shift_rows(left, -1) + beta * ends_ref[BLOCKS : 2 * BLOCKS]
     give_ref[:, 0, 2 * LANES : 3 * LANES] = shift_rows(take_ref[:, 0, 2 * LANES : 3 * LANES], 1)
     give_ref[:, 0, 3 * LANES :] = shift_rows(take_ref[:, 0, 3 * LANES :], -1)
     wait(fetch([(give_ref, give_hbm)], sems))
 
 
 def part_kernel(
-    force_hbm, radii_hbm, mix_hbm, part_hbm, mixed_hbm, force_ref, radii_ref, mix_ref, part_ref, mixed_ref, sems
+    index_ref, force_hbm, radii_hbm, mix_hbm, part_hbm, mixed_hbm, ends_ref,
+    force_ref, radii_ref, mix_ref, part_ref, mixed_ref, sems,
 ):
     copies = fetch([(radii_hbm, radii_ref), (mix_hbm, mix_ref), (force_hbm, force_ref)], sems)
     wait(copies[:2])
+    me = index_ref[0]
+    rho, _ = decay_of(eigen_values(me // NL * LANES, LANES) + radii_ref[me % NL])
+    rate = rho
+    for _ in range(3):
+        rate = rate * rate
+    place = iota((BLOCKS, LANES), 0)
+    power = jnp.ones((BLOCKS, LANES), jnp.float32)
+    reverse = power
+    for bit in range(8):
+        ends_ref[2 * BLOCKS + bit : 2 * BLOCKS + bit + 1] = rate
+        if bit < 7:
+            odd = (place >> bit) % 2 == 1
+            power = power * jnp.where(odd, rate, 1.0)
+            reverse = reverse * jnp.where(odd, 1.0, rate)
+        rate = rate * rate
+    ends_ref[2 * BLOCKS + 8 : 2 * BLOCKS + 9] = rho
+    ends_ref[:BLOCKS] = power
+    ends_ref[BLOCKS : 2 * BLOCKS] = reverse
     tall = NL * TALL
     row = iota((tall, NL), 0)
     layer = jnp.where(row < NL * ROWS, row // ROWS, row % NL)
@@ -218,6 +230,7 @@
     mixed_ref[...] = jnp.where(iota((tall, tall), 1) // NL == place, mixed, 0.0)
     written = fetch([(mixed_ref, mixed_hbm)], sems, 3)
     rho, _ = mode_decay(radii_ref)
+    part_ref[TALL] = rho
     wait(copies[2:])
     right = jnp.zeros((NL, N), jnp.float32)
     for y in range(ROWS):
@@ -298,22 +311,17 @@
 
 
 def backward_kernel(
-    index_ref, take_ref, part_ref, mixed_ref, radii_hbm, high_hbm, low_hbm, coef_hbm, vortex_hbm, stream_hbm,
-    radii_ref, high_ref, low_ref, coef_ref, psi_ref, south_ref, north_ref, wave_ref, vortex_ref, stream_ref, sems,
+    index_ref, take_ref, part_ref, mixed_ref, table_ref, coef_hbm, vortex_hbm, stream_hbm, coef_ref, psi_ref, south_ref, north_ref, wave_ref, vortex_ref, stream_ref, sems,
 ):
-    copies = fetch(
-        [(radii_hbm, radii_ref), (high_hbm, high_ref), (low_hbm, low_ref), (coef_hbm, coef_ref)], sems
-    )
+    copies = fetch([(coef_hbm.at[i], coef_ref.at[i]) for i in (NL, *range(NL))], sems)
     out = len(copies)
-    copies[0].wait()
-    rho, _ = mode_decay(radii_ref)
     for c in range(N // LANES):
         cols = slice(c * LANES, (c + 1) * LANES)
         up = take_ref[c * NL : (c + 1) * NL, 0, :LANES]
         down = take_ref[c * NL : (c + 1) * NL, 0, LANES : 2 * LANES]
         south_ref[:, cols] = take_ref[c * NL : (c + 1) * NL, 0, 2 * LANES : 3 * LANES]
         north_ref[:, cols] = take_ref[c * NL : (c + 1) * NL, 0, 3 * LANES :]
-        near = rho[:, cols]
+        near = part_ref[TALL, :, cols]
         ups, downs = [up], [down]
         for _ in range(ROWS + 1):
             ups.append(ups[-1] * near)
@@ -321,16 +329,19 @@
         for i in range(TALL):
             psi_ref[i * NL : (i + 1) * NL, cols] = part_ref[i, :, cols] + ups[i] + downs[ROWS + 1 - i]
     split = halves(split_dot(halves(mixed_ref[...]), halves(psi_ref[...])))
-    wait(copies[1:3])
-    for n in range(PIECES):
-        wave_ref[:, n * STEP : (n + 1) * STEP] = split_dot(split, (high_ref[n], low_ref[n]))
+    sums = []
+    for odd in range(2):
+        some = tuple(part[:, odd * HALF : (odd + 1) * HALF] for part in split)
+        sums.append(split_dot(some, (table_ref[odd, 0], table_ref[odd, 1]), 1))
+    wave_ref[:, :HALF] = sums[0] + sums[1]
+    wave_ref[:, HALF:] = mirrored(sums[0] - sums[1])
     inside_low = jnp.where(index_ref[0] > 0, 1.0, 0.0)
     inside_high = jnp.where(index_ref[0] < BLOCKS - 1, 1.0, 0.0)
     body = NL * ROWS
     for layer in range(NL):
         stream_ref[layer] = wave_ref[layer * ROWS : (layer + 1) * ROWS]
     written = fetch([(stream_ref, stream_hbm)], sems, out)
-    wait(copies[3:])
+    copies[0].wait()
     twelfth = coef_ref[NL, 1]
     for y, edge_ref, beyond, sign in (
         (0, south_ref, inside_low * wave_ref[body : body + NL], 1.0),
@@ -341,8 +352,9 @@
         east, west = roll_lanes(edge, -1), roll_lanes(edge, 1)
         more = roll_lanes(here, -1) * (edge + east) - roll_lanes(here, 1) * (edge + west)
         more += edge * (roll_lanes(beyond, -1) - roll_lanes(beyond, 1)) - beyond * (east - west)
-        coef_ref[:NL, 8, y] += sign * twelfth[y : y + 1] * more
+        edge_ref[...] = sign * twelfth[y : y + 1] * more
     for layer in range(NL):
+        copies[1 + layer].wait()
         mid = wave_ref[layer * ROWS : (layer + 1) * ROWS]
         north = roll_sub(mid, inside_high * wave_ref[body + NL + layer : body + NL + layer + 1], -1)
         south = roll_sub(mid, inside_low * wave_ref[body + layer : body + layer + 1], 1)
@@ -353,12 +365,14 @@
         from_west = coef_ref[layer, 5] * mid + coef_ref[layer, 6] * north + coef_ref[layer, 7] * south
         vortex_ref[layer] = total + pltpu.roll(from_east, N - 1, 1) + pltpu.roll(from_west, 1, 1)
         if layer % 4 == 3:
-            some = pl.ds(layer - 3, 4)
+            some = slice(layer - 3, layer + 1)
+            vortex_ref[some, 0] += south_ref[some]
+            vortex_ref[some, ROWS - 1] += north_ref[some]
             written += fetch([(vortex_ref.at[some], vortex_hbm.at[some])], sems, out + 1 + layer // 4)
     wait(written)
 
 
-def call(kernel, outs, args, scratch, flops, nbytes, scalars=(), near=(), limit=60 * 1024 * 1024):
+def call(kernel, outs, args, scratch, flops, nbytes, scalars=(), near=(), limit=60 * 1024 * 1024, kept=0):
     def room(kind):
         return pltpu.VMEM(*kind) if isinstance(kind, tuple) else kind
 
@@ -366,7 +380,7 @@
         kernel,
         out_shape=[jax.ShapeDtypeStruct(s, d) for s, d in outs],
         in_specs=[SMEM] * len(scalars) + [VMEM] * len(near) + [ANY] * len(args),
-        out_specs=[ANY] * len(outs),
+        out_specs=[ANY] * (len(outs) - kept) + [VMEM] * kept,
         scratch_shapes=[room(kind) for kind in scratch],
         compiler_params=pltpu.CompilerParams(vmem_limit_bytes=limit),
         cost_estimate=pl.CostEstimate(flops=flops, bytes_accessed=nbytes, transcendentals=0),
@@ -378,29 +392,30 @@
     plane = ((ROWS, N), f32)
     edge = ((NL, N), f32)
     mixing = ((NL, NL), f32)
-    sines = ((PIECES, N, STEP), bf16)
+    sines = ((2, 2, HALF, HALF), bf16)
     packet = ((BLOCKS, 1, 4 * LANES), f32)
     rows = ((ROWS, NL, N), f32)
     rates = pltpu.SMEM((NL,), f32)
-    parts = [((TALL, NL, N), f32), ((NL * TALL, NL * TALL), f32)]
+    parts = [((TALL + 1, NL, N), f32), ((NL * TALL, NL * TALL), f32)]
+    ends = ((2 * BLOCKS + 16, LANES), f32)
     weights = ((NL + 1, 9, ROWS, N), f32)
     wave = ((NL * TALL, N), f32)
 
     index = (lax.axis_index("group") * lax.axis_size("tile") + lax.axis_index("tile")).astype(i32).reshape(1)
-    outs = [packet, rows, sines, sines]
-    send, force, high, low = call(
-        forward_kernel, outs, (vorticity, layer_to_mode, inverse_radii, jnp.asarray(host_table())),
-        [field, mixing, rates, ((4, 32, N), f32), *outs, DMA((5 + 3 * PIECES,))],
+    outs = [packet, rows]
+    table = jnp.asarray(host_table())
+    send, force = call(
+        forward_kernel, outs, (vorticity, layer_to_mode, inverse_radii, table),
+        [field, mixing, rates, sines, *outs, DMA((6 + PIECES,))],
         6 * 128 * N * N, 6 << 20,
     )
     take = lax.all_to_all(send, AXES, split_axis=0, concat_axis=0, tiled=True)
-    part, mixed = call(
-        part_kernel, parts, (force, inverse_radii, mode_to_layer), [rows, rates, mixing, *parts, DMA((5,))],
-        1 << 24, 1 << 20,
+    part, mixed, ends = call(
+        part_kernel, parts + [ends], (force, inverse_radii, mode_to_layer), [rows, rates, mixing, *parts, DMA((5,))],
+        1 << 24, 1 << 20, [index], limit=50000 << 10, kept=1,
     )
     (give,) = call(
-        scan_kernel, [packet], (inverse_radii, part), [rates, packet, DMA((1,))],
-        1 << 22, 1 << 18, [index], [take], limit=54500 << 10,
+        scan_kernel, [packet], (), [packet, DMA((1,))], 1 << 22, 1 << 18, (), [take, ends], limit=54500 << 10,
     )
     amplitude = lax.all_to_all(give, AXES, split_axis=0, concat_axis=0, tiled=True)
     (coef,) = call(
@@ -411,9 +426,9 @@
     return tuple(
         call(
             backward_kernel, [field, field],
-            (inverse_radii, high, low, coef),
-            [rates, sines, sines, weights, wave, edge, edge, wave, field, field, DMA((9,))],
-            6 * 160 * N * N, 10 << 20, [index], [amplitude, part, mixed], limit=53500 << 10,
+            (coef,),
+            [weights, wave, edge, edge, wave, field, field, DMA((NL + 6,))],
+            6 * 160 * N * N, 10 << 20, [index], [amplitude, part, mixed, table], limit=51500 << 10,
         )
     )
 

time: 50.9 us -> 48.5 us (0.953)
  Pallas kernels: 18.7 us -> 16 us
  local copies, waits for them, and re-layouts: 0.01 us -> 2.39 us
  waiting for transfers between devices: 15.8 us -> 13.7 us
    pallas_call x5, Pallas kernels: 18.7 us -> 16 us  [call(): pl.pallas_call(kernel, out_shape=[jax.ShapeDtypeStruct(s, d) for s, d in...]
    unnamed x6 -> x8, local copies, waits for them, and re-layouts: 0.01 us -> 2.39 us
    all_to_all x1, waiting for transfers between devices: 9.19 us -> 6.98 us  [body(): take = lax.all_to_all(send, AXES, split_axis=0, concat_axis=0, tiled=True)]
where the time goes in v3:
time: 48.5 us; the launch traced here: 48.2 us
  Pallas kernels  16 us (33%)
  starting transfers between devices  15.3 us (32%)
  waiting for transfers between devices  13.7 us (28%)
  local copies, waits for them, and re-layouts  2.39 us (5%)
  between operations  0.7 us (1%)
    pallas_call x5, Pallas kernels, call(): pl.pallas_call(kernel, out_shape=[jax.ShapeDtypeStruct(s, d) for s, d in...  16 us
    all_to_all x1, starting transfers between devices, body(): take = lax.all_to_all(send, AXES, split_axis=0, concat_axis=0, tiled=True)  11.5 us
    all_to_all x1, waiting for transfers between devices, body(): take = lax.all_to_all(send, AXES, split_axis=0, concat_axis=0, tiled=True)  6.98 us
    all_to_all x1, waiting for transfers between devices, body(): lax.all_to_all(give, AXES, split_axis=0, concat_axis=0, tiled=True)  6.75 us
    all_to_all x1, starting transfers between devices, body(): lax.all_to_all(give, AXES, split_axis=0, concat_axis=0, tiled=True)  3.82 us
    unnamed x8, local copies, waits for them, and re-layouts  2.39 us
  transfers between devices with their start and end apart: 2, of which 2 were waited for; matrix products, arithmetic and copies ran while one was open for 0% of the time, Pallas kernels for 14%

profile of v3, /device:TPU:1, one launch (start us, length us, event | category | flops | bytes accessed | tf_op | source)
XLA Modules:
  0.0 48.2 jit_solution(12963104359329542755)
XLA Ops:
  0.6 0.0 copy-start
  0.6 3.6 %shard_map.86 = (f32[128,1,512]{2,1,0:T(1,128)}, f32[8,16,1024]{2,1,0:T(8,128)}) custom-call(f32[16,8,1024]{2,1,0:T(8,128)} %vortex_hbm.3, f32[16,16]{1,0:T(8,128)} %mix_hbm.2, f32[16]{0:T(128)} %radii_hbm.3, bf16[2,2,512,512]{3,2,1,0:T(8,128)(2,1)} %constant.13.clone.table_hbm.table_ref), custom_call_target="tpu_custom_call" | custom-call | flops 805306368 | bytes 6291456 | tf_op jit(solution)/shard_map/pallas_call | solution.py:379
  4.3 11.5 %all-to-all-start = ((f32[128,1,512]{2,1,0:T(1,128)}), f32[128,1,512]{2,1,0:T(1,128)S(1)}, u32[]{:S(2)}, u32[]{:S(2)}) async-start(f32[128,1,512]{2,1,0:T(1,128)} %get-tuple-element.7), calls=%async_computation | async-start | bytes 524288 | tf_op jit(solution)/shard_map/all_to_all | solution.py:412
  15.8 0.0 copy-start.1
  15.8 1.0 %copy-done.1 = f32[8,16,1024]{2,1,0:T(8,128)S(1)} copy-done((f32[8,16,1024]{2,1,0:T(8,128)S(1)}, f32[8,16,1024]{2,1,0:T(8,128)}, u32[]{:S(2)}) %copy-start.1) | copy-done | bytes 524312
  16.8 0.0 copy-start.2
  16.8 0.7 %copy-done.2 = f32[16,16]{1,0:T(8,128)S(1)} copy-done((f32[16,16]{1,0:T(8,128)S(1)}, f32[16,16]{1,0:T(8,128)}, u32[]{:S(2)}) %copy-start.2) | copy-done | bytes 1048
  17.5 0.0 copy-start.3
  17.5 0.7 %copy-done.3 = f32[16]{0:T(128)S(1)} copy-done((f32[16]{0:T(128)S(1)}, f32[16]{0:T(128)}, u32[]{:S(2)}) %copy-start.3) | copy-done | bytes 88
  18.2 2.1 %shard_map.87 = (f32[11,16,1024]{2,1,0:T(8,128)S(1)}, f32[160,160]{1,0:T(8,128)S(1)}, f32[272,128]{1,0:T(8,128)S(1)}) custom-call(s32[1]{0:T(128)} %bitcast.index_ref, f32[8,16,1024]{2,1,0:T(8,128)S(1)} %copy-done.1, f32[16]{0:T(128)S(1)} %copy-done.3, f32[16,16]{1,0:T(8,128)S(1)} %copy-done.2), custom_call_target="tpu_custom_call" | custom-call | flops 16777216 | bytes 1048576 | tf_op jit(solution)/shard_map/pallas_call | solution.py:379
  20.3 7.0 %all-to-all-done.take_ref = f32[128,1,512]{2,1,0:T(1,128)S(1)} async-done(((f32[128,1,512]{2,1,0:T(1,128)}), f32[128,1,512]{2,1,0:T(1,128)S(1)}, u32[]{:S(2)}, u32[]{:S(2)}) %all-to-all-start) | async-done | bytes 262176 | tf_op jit(solution)/shard_map/all_to_all | solution.py:412
  27.2 1.2 %shard_map.88.after_hbm = f32[128,1,512]{2,1,0:T(1,128)} custom-call(f32[128,1,512]{2,1,0:T(1,128)S(1)} %all-to-all-done.take_ref, f32[272,128]{1,0:T(8,128)S(1)} %get-tuple-element.9.ends_ref), custom_call_target="tpu_custom_call" | custom-call | flops 4194304 | bytes 262144 | tf_op jit(solution)/shard_map/pallas_call | solution.py:379
  28.4 3.8 %all-to-all-start.1 = ((f32[128,1,512]{2,1,0:T(1,128)}), f32[128,1,512]{2,1,0:T(1,128)S(1)}, u32[]{:S(2)}, u32[]{:S(2)}) async-start(f32[128,1,512]{2,1,0:T(1,128)} %shard_map.88.after_hbm), calls=%async_computation.1 | async-start | bytes 524288 | tf_op jit(solution)/shard_map/all_to_all | solution.py:420
  32.2 4.9 %shard_map.89.coef_hbm = f32[17,9,8,1024]{3,2,1,0:T(8,128)} custom-call(f32[16,8,1024]{2,1,0:T(8,128)} %vortex_hbm.3, f32[8,1024]{1,0:T(8,128)} %wind_hbm.1, s32[8,1024]{1,0:T(8,128)} %wet_hbm.1, f32[128,1,512]{2,1,0:T(1,128)} %shard_map.88.after_hbm), custom_call_target="tpu_custom_call" | custom-call | flops 16777216 | bytes 5242880 | tf_op jit(solution)/shard_map/pallas_call | solution.py:379
  37.1 6.7 %all-to-all-done.1.take_ref = f32[128,1,512]{2,1,0:T(1,128)S(1)} async-done(((f32[128,1,512]{2,1,0:T(1,128)}), f32[128,1,512]{2,1,0:T(1,128)S(1)}, u32[]{:S(2)}, u32[]{:S(2)}) %all-to-all-start.1) | async-done | bytes 262176 | tf_op jit(solution)/shard_map/all_to_all | solution.py:420
  43.9 0.0 copy-done
  43.9 4.3 %shard_map.90 = (f32[16,8,1024]{2,1,0:T(8,128)}, f32[16,8,1024]{2,1,0:T(8,128)}) custom-call(s32[1]{0:T(128)} %bitcast.index_ref, f32[128,1,512]{2,1,0:T(1,128)S(1)} %all-to-all-done.1.take_ref, f32[11,16,1024]{2,1,0:T(8,128)S(1)} %get-tuple-element.10.part_ref, f32[160,160]{1,0:T(8,128)S(1)} %get-tuple-element.11.mixed_ref, ...), custom_call_target="tpu_custom_call" | custom-call | flops 1006632960 | bytes 10485760 | tf_op jit(solution)/shard_map/pallas_call | solution.py:379
Async XLA Ops:
  0.6 43.2 %copy-start = (bf16[2,2,512,512]{3,2,1,0:T(8,128)(2,1)S(1)}, bf16[2,2,512,512]{3,2,1,0:T(8,128)(2,1)}, u32[]{:S(2)}) copy-start(bf16[2,2,512,512]{3,2,1,0:T(8,128)(2,1)} %constant.13.clone.table_hbm.table_ref) | copy-start | bytes 6291460
  4.3 23.0 %all-to-all-start = ((f32[128,1,512]{2,1,0:T(1,128)}), f32[128,1,512]{2,1,0:T(1,128)S(1)}, u32[]{:S(2)}, u32[]{:S(2)}) async-start(f32[128,1,512]{2,1,0:T(1,128)} %get-tuple-element.7), calls=%async_computation | async-start | bytes 524288 | tf_op jit(solution)/shard_map/all_to_all | solution.py:412
  15.8 1.0 %copy-start.1 = (f32[8,16,1024]{2,1,0:T(8,128)S(1)}, f32[8,16,1024]{2,1,0:T(8,128)}, u32[]{:S(2)}) copy-start(f32[8,16,1024]{2,1,0:T(8,128)} %get-tuple-element.8.force_hbm) | copy-start | bytes 1572868
  16.8 0.7 %copy-start.2 = (f32[16,16]{1,0:T(8,128)S(1)}, f32[16,16]{1,0:T(8,128)}, u32[]{:S(2)}) copy-start(f32[16,16]{1,0:T(8,128)} %mix_hbm.3) | copy-start | bytes 3076
  17.5 0.7 %copy-start.3 = (f32[16]{0:T(128)S(1)}, f32[16]{0:T(128)}, u32[]{:S(2)}) copy-start(f32[16]{0:T(128)} %radii_hbm.3) | copy-start | bytes 196
  28.4 15.4 %all-to-all-start.1 = ((f32[128,1,512]{2,1,0:T(1,128)}), f32[128,1,512]{2,1,0:T(1,128)S(1)}, u32[]{:S(2)}, u32[]{:S(2)}) async-start(f32[128,1,512]{2,1,0:T(1,128)} %shard_map.88.after_hbm), calls=%async_computation.1 | async-start | bytes 524288 | tf_op jit(solution)/shard_map/all_to_all | solution.py:420

commit v4 on v3

--- a/solution.py
+++ b/solution.py
@@ -113,38 +113,39 @@
 
 
 def forward_kernel(
-    vortex_hbm, mix_hbm, radii_hbm, table_hbm,
-    send_hbm, force_hbm,
-    vortex_ref, mix_ref, radii_ref, table_ref, send_ref, force_ref, sems,
+    vortex_hbm, mix_hbm, back_hbm, radii_hbm, table_hbm,
+    send_hbm, carry_hbm,
+    vortex_ref, mix_ref, back_ref, radii_ref, table_ref, send_ref, force_ref, sems,
 ):
-    copies = fetch(
-        [
-            (mix_hbm, mix_ref), (radii_hbm, radii_ref), (vortex_hbm, vortex_ref),
-            (table_hbm.at[0], table_ref.at[0]), (table_hbm.at[1], table_ref.at[1]),
-        ],
-        sems,
-    )
+    copies = fetch([(mix_hbm, mix_ref), (radii_hbm, radii_ref)], sems)
+    layers = [pl.ds(i, 4) for i in range(0, NL, 4)]
+    loads = fetch([(vortex_hbm.at[some], vortex_ref.at[some]) for some in layers], sems, 2)
+    copies += fetch([(back_hbm, back_ref)], sems, 6)
+    places = [(odd, low, pl.ds(i, STEP)) for odd in range(2) for low in range(2) for i in range(0, HALF, STEP)]
+    waves = fetch([(table_hbm.at[place], table_ref.at[place]) for place in places], sems, 7)
     rows = NL * ROWS
     spread = (iota((NL, rows), 1) // ROWS == iota((NL, rows), 0)).astype(jnp.float32)
     wait(copies[:2])
     rho, weight = mode_decay(radii_ref)
+    force_ref[2 * ROWS : 2 * ROWS + 2] = rho.reshape(2, ROWS, N)
     wide = dot(mix_ref[...], spread, HIGHEST)
     mix = jnp.concatenate([wide] * ROWS, 0)
     mix = jnp.where(iota((rows, rows), 0) // NL == iota((rows, rows), 1) % ROWS, mix, 0.0)
-    wait(copies[2:3])
+    wait(loads)
     written = []
-    for c in range(N // LANES):
-        part = slice(c * LANES, (c + 1) * LANES)
-        send_ref[c * NL : (c + 1) * NL, 0, 2 * LANES : 3 * LANES] = vortex_ref[:, ROWS - 1, part]
-        send_ref[c * NL : (c + 1) * NL, 0, 3 * LANES :] = vortex_ref[:, 0, part]
-    modal = split_dot(halves(mix), halves(vortex_ref[...].reshape(rows, N)))
+    high, low = halves(mix)
+    mix = jnp.concatenate([jnp.concatenate([high, high], 1), jnp.concatenate([low, jnp.zeros_like(low)], 1)], 0)
+    modal = dot(mix, jnp.concatenate(halves(vortex_ref[...].reshape(rows, N)), 0))
+    modal = modal[:rows] + modal[rows:]
     mirror = mirrored(modal[:, HALF:])
     folded = [halves(modal[:, :HALF] + mirror), halves(modal[:, :HALF] - mirror)]
     for n in range(PIECES):
         cols = slice(n * STEP, (n + 1) * STEP)
         odd, start = divmod(n * STEP, HALF)
         if start == 0:
-            copies[3 + odd].wait()
+            wait(waves[4 * odd : 4 * odd + 4])
+            if odd:
+                written += fetch([(vortex_ref, carry_hbm.at[pl.ds(2 * TALL, NL)])], sems, 16 + PIECES)
         some = slice(start, start + STEP)
         spectrum = split_dot(folded[odd], (table_ref[odd, 0, :, some], table_ref[odd, 1, :, some]))
         right = jnp.zeros((NL, STEP), jnp.float32)
@@ -152,7 +153,7 @@
         force = []
         for y in range(ROWS):
             force.append(-weight[:, cols] * spectrum[y * NL : (y + 1) * NL])
-            force_ref[y, :, cols] = force[y]
+            force_ref[2 * y : 2 * y + 2, :, cols] = force[y].reshape(2, ROWS, STEP)
             right = rho[:, cols] * right + force[y]
         for y in reversed(range(ROWS)):
             left = rho[:, cols] * left + force[y]
@@ -161,9 +162,14 @@
             part = slice(c * LANES, (c + 1) * LANES)
             send_ref[dest * NL : (dest + 1) * NL, 0, :LANES] = right[:, part]
             send_ref[dest * NL : (dest + 1) * NL, 0, LANES : 2 * LANES] = left[:, part]
+            part = slice(dest * LANES, (dest + 1) * LANES)
+            send_ref[dest * NL : (dest + 1) * NL, 0, 2 * LANES : 3 * LANES] = vortex_ref[:, ROWS - 1, part]
+            send_ref[dest * NL : (dest + 1) * NL, 0, 3 * LANES :] = vortex_ref[:, 0, part]
         dests = pl.ds(n * (STEP // LANES) * NL, STEP // LANES * NL)
-        written += fetch([(send_ref.at[dests], send_hbm.at[dests])], sems, 5 + n)
-    written += fetch([(force_ref, force_hbm)], sems, 5 + PIECES)
+        written += fetch([(send_ref.at[dests], send_hbm.at[dests])], sems, 15 + n)
+    wait(copies[2:])
+    force_ref[2 * ROWS + 2 :, :, :NL] = back_ref[...].reshape(2, ROWS, NL)
+    written += fetch([(force_ref, carry_hbm.at[pl.ds(0, 2 * TALL)])], sems, 15 + PIECES)
     wait(written)
 
 
@@ -196,13 +202,13 @@
 
 
 def part_kernel(
-    index_ref, force_hbm, radii_hbm, mix_hbm, part_hbm, mixed_hbm, ends_ref,
-    force_ref, radii_ref, mix_ref, part_ref, mixed_ref, sems,
+    index_ref, carry_hbm, part_ref, mixed_ref, ends_ref, force_ref, sems
 ):
-    copies = fetch([(radii_hbm, radii_ref), (mix_hbm, mix_ref), (force_hbm, force_ref)], sems)
-    wait(copies[:2])
+    wait(fetch([(carry_hbm.at[pl.ds(0, 2 * TALL)], force_ref)], sems))
     me = index_ref[0]
-    rho, _ = decay_of(eigen_values(me // NL * LANES, LANES) + radii_ref[me % NL])
+    here = pl.ds(pl.multiple_of(me // NL * LANES, LANES), LANES)
+    every = force_ref[2 * ROWS : 2 * ROWS + 2, :, here].reshape(NL, LANES)
+    rho = jnp.sum(jnp.where(iota((NL, LANES), 0) == me % NL, every, 0.0), 0, keepdims=True)
     rate = rho
     for _ in range(3):
         rate = rate * rate
@@ -224,25 +230,23 @@
     layer = jnp.where(row < NL * ROWS, row // ROWS, row % NL)
     pick = (layer == iota((tall, NL), 1)).astype(jnp.float32)
     wide = (iota((NL, tall), 1) % NL == iota((NL, tall), 0)).astype(jnp.float32)
-    mixed = dot(dot(pick, mix_ref[...], HIGHEST), wide, HIGHEST)
+    mixed = dot(dot(pick, force_ref[2 * ROWS + 2 :, :, :NL].reshape(NL, NL), HIGHEST), wide, HIGHEST)
     row = iota((tall, tall), 0)
     place = jnp.where(row < NL * ROWS, row % ROWS + 1, jnp.where(row < NL * (ROWS + 1), 0, ROWS + 1))
     mixed_ref[...] = jnp.where(iota((tall, tall), 1) // NL == place, mixed, 0.0)
-    written = fetch([(mixed_ref, mixed_hbm)], sems, 3)
-    rho, _ = mode_decay(radii_ref)
+    force = [force_ref[2 * y : 2 * y + 2].reshape(NL, N) for y in range(ROWS + 1)]
+    rho = force[ROWS]
     part_ref[TALL] = rho
-    wait(copies[2:])
     right = jnp.zeros((NL, N), jnp.float32)
     for y in range(ROWS):
-        right = rho * right + force_ref[y]
+        right = rho * right + force[y]
         part_ref[y + 1] = right
     part_ref[ROWS + 1] = rho * right
     left = jnp.zeros((NL, N), jnp.float32)
     for y in reversed(range(ROWS)):
         part_ref[y + 1] += left
-        left = rho * (left + force_ref[y])
+        left = rho * (left + force[y])
     part_ref[0] = left
-    wait(written + fetch([(part_ref, part_hbm)], sems, 4))
 
 
 def roll_lanes(value, step):
@@ -259,62 +263,18 @@
     return jnp.where(sub == (0 if step > 0 else height - 1), edge, rolled)
 
 
-def weight_kernel(
-    vortex_hbm, wind_hbm, wet_hbm, after_hbm, coef_hbm, vortex_ref, wind_ref, wet_ref, coef_ref, sems
+def difference(value):
+    return roll_lanes(value, -1) - roll_lanes(value, 1)
+
+
+def backward_kernel(
+    index_ref, take_ref, part_ref, mixed_ref, table_ref, wet_ref, wind_ref, carry_hbm, vortex_hbm, stream_hbm, given_ref, psi_ref,
+    south_ref, north_ref, edge_ref, wave_ref, vortex_ref, stream_ref, sems,
 ):
-    del after_hbm
-    wait(
-        fetch(
-            [(wet_hbm, wet_ref), (wind_hbm, wind_ref), (vortex_hbm, vortex_ref)], sems
-        )
-    )
-    keep = time_step * wet_ref[...].astype(jnp.float32)
-    twelfth = keep * (1.0 / 12.0)
-    written = []
-    for layer in range(NL):
-        mid = vortex_ref[layer]
-        north = roll_sub(mid, 0.0, -1)
-        south = roll_sub(mid, 0.0, 1)
-        east = roll_lanes(mid, -1)
-        west = roll_lanes(mid, 1)
-        north_east = roll_lanes(north, -1)
-        north_west = roll_lanes(north, 1)
-        south_east = roll_lanes(south, -1)
-        south_west = roll_lanes(south, 1)
-        along = north - south
-        across = east - west
-        c_east = -twelfth * (along + (north_east - south_east)) - keep * (0.5 * beta_plane)
-        c_west = twelfth * (along + (north_west - south_west)) + keep * (0.5 * beta_plane)
-        c_north = twelfth * (across + (north_east - north_west))
-        c_south = -twelfth * (across + (south_east - south_west))
-        if layer == NL - 1:
-            drag = keep * bottom_drag
-            c_east = c_east - drag
-            c_west = c_west - drag
-            c_north = c_north - drag
-            c_south = c_south - drag
-            coef_ref[NL, 0] = 4.0 * drag
-            coef_ref[NL, 1] = twelfth
-        coef_ref[layer, 0] = c_north
-        coef_ref[layer, 1] = c_south
-        coef_ref[layer, 2] = roll_lanes(c_east, 1)
-        coef_ref[layer, 3] = roll_lanes(-twelfth * (north - east), 1)
-        coef_ref[layer, 4] = roll_lanes(twelfth * (south - east), 1)
-        coef_ref[layer, 5] = roll_lanes(c_west, -1)
-        coef_ref[layer, 6] = roll_lanes(twelfth * (north - west), -1)
-        coef_ref[layer, 7] = roll_lanes(-twelfth * (south - west), -1)
-        coef_ref[layer, 8] = mid + keep * wind_ref[...] if layer == 0 else mid
-        if layer % 4 == 3:
-            some = pl.ds(layer - 3, 4 if layer < NL - 1 else 5)
-            written += fetch([(coef_ref.at[some], coef_hbm.at[some])], sems, 3 + layer // 4)
-    wait(written)
-
-
-def backward_kernel(
-    index_ref, take_ref, part_ref, mixed_ref, table_ref, coef_hbm, vortex_hbm, stream_hbm, coef_ref, psi_ref, south_ref, north_ref, wave_ref, vortex_ref, stream_ref, sems,
-):
-    copies = fetch([(coef_hbm.at[i], coef_ref.at[i]) for i in (NL, *range(NL))], sems)
-    out = len(copies)
+    loads = fetch(
+        [(carry_hbm.at[pl.ds(2 * TALL + i, 4)], given_ref.at[pl.ds(i, 4)]) for i in range(0, NL, 4)], sems
+    )
+    out = len(loads)
     for c in range(N // LANES):
         cols = slice(c * LANES, (c + 1) * LANES)
         up = take_ref[c * NL : (c + 1) * NL, 0, :LANES]
@@ -341,33 +301,40 @@
     for layer in range(NL):
         stream_ref[layer] = wave_ref[layer * ROWS : (layer + 1) * ROWS]
     written = fetch([(stream_ref, stream_hbm)], sems, out)
-    copies[0].wait()
-    twelfth = coef_ref[NL, 1]
-    for y, edge_ref, beyond, sign in (
-        (0, south_ref, inside_low * wave_ref[body : body + NL], 1.0),
-        (ROWS - 1, north_ref, inside_high * wave_ref[body + NL :], -1.0),
-    ):
-        here = stream_ref[:, y]
-        edge = edge_ref[...]
-        east, west = roll_lanes(edge, -1), roll_lanes(edge, 1)
-        more = roll_lanes(here, -1) * (edge + east) - roll_lanes(here, 1) * (edge + west)
-        more += edge * (roll_lanes(beyond, -1) - roll_lanes(beyond, 1)) - beyond * (east - west)
-        edge_ref[...] = sign * twelfth[y : y + 1] * more
+    wait(loads)
+    keep = time_step * wet_ref[...].astype(jnp.float32)
+    twelfth = keep * (1.0 / 12.0)
+    edges = [inside_low * wave_ref[body : body + NL], inside_high * wave_ref[body + NL :], south_ref[...], north_ref[...]]
+    for i, edge in enumerate(edges):
+        edge_ref[2 * i] = edge
+        edge_ref[2 * i + 1] = difference(edge)
     for layer in range(NL):
-        copies[1 + layer].wait()
-        mid = wave_ref[layer * ROWS : (layer + 1) * ROWS]
-        north = roll_sub(mid, inside_high * wave_ref[body + NL + layer : body + NL + layer + 1], -1)
-        south = roll_sub(mid, inside_low * wave_ref[body + layer : body + layer + 1], 1)
-        total = coef_ref[layer, 8] + coef_ref[layer, 0] * north + coef_ref[layer, 1] * south
+        below, across_below, above, across_above, old_below, old_across_below, old_above, old_across_above = (
+            edge_ref[i, layer : layer + 1] for i in range(8)
+        )
+        old = given_ref[layer]
+        old_across = difference(old)
+        old_north = roll_sub(old, old_above, -1)
+        old_south = roll_sub(old, old_below, 1)
+        mid = stream_ref[layer]
+        east, west = roll_lanes(mid, -1), roll_lanes(mid, 1)
+        across = east - west
+        north = roll_sub(mid, above, -1)
+        south = roll_sub(mid, below, 1)
+        along = north - south
+        mixture = (old_north - old_south + 12.0 * 0.5 * beta_plane) * mid - old * along
+        total = old_south * (across + roll_sub(across, across_below, 1))
+        total -= old_north * (across + roll_sub(across, across_above, -1))
+        total += old_across * along - difference(mixture)
+        total += roll_sub(old_across, old_across_above, -1) * north - roll_sub(old_across, old_across_below, 1) * south
+        total = old + twelfth * total
+        if layer == 0:
+            total += keep * wind_ref[...]
         if layer == NL - 1:
-            total = total + coef_ref[NL, 0] * mid
-        from_east = coef_ref[layer, 2] * mid + coef_ref[layer, 3] * north + coef_ref[layer, 4] * south
-        from_west = coef_ref[layer, 5] * mid + coef_ref[layer, 6] * north + coef_ref[layer, 7] * south
-        vortex_ref[layer] = total + pltpu.roll(from_east, N - 1, 1) + pltpu.roll(from_west, 1, 1)
+            total -= (bottom_drag * keep) * (north + south + east + west - 4.0 * mid)
+        vortex_ref[layer] = total
         if layer % 4 == 3:
             some = slice(layer - 3, layer + 1)
-            vortex_ref[some, 0] += south_ref[some]
-            vortex_ref[some, ROWS - 1] += north_ref[some]
             written += fetch([(vortex_ref.at[some], vortex_hbm.at[some])], sems, out + 1 + layer // 4)
     wait(written)
 
@@ -394,41 +361,34 @@
     mixing = ((NL, NL), f32)
     sines = ((2, 2, HALF, HALF), bf16)
     packet = ((BLOCKS, 1, 4 * LANES), f32)
-    rows = ((ROWS, NL, N), f32)
+    rows = ((2 * TALL, ROWS, N), f32)
+    carry = ((112, ROWS, N), f32)
     rates = pltpu.SMEM((NL,), f32)
     parts = [((TALL + 1, NL, N), f32), ((NL * TALL, NL * TALL), f32)]
     ends = ((2 * BLOCKS + 16, LANES), f32)
-    weights = ((NL + 1, 9, ROWS, N), f32)
     wave = ((NL * TALL, N), f32)
 
     index = (lax.axis_index("group") * lax.axis_size("tile") + lax.axis_index("tile")).astype(i32).reshape(1)
-    outs = [packet, rows]
+    outs = [packet, carry]
     table = jnp.asarray(host_table())
-    send, force = call(
-        forward_kernel, outs, (vorticity, layer_to_mode, inverse_radii, table),
-        [field, mixing, rates, sines, *outs, DMA((6 + PIECES,))],
-        6 * 128 * N * N, 6 << 20,
+    send, kept = call(
+        forward_kernel, outs, (vorticity, layer_to_mode, mode_to_layer, inverse_radii, table),
+        [field, mixing, mixing, rates, sines, packet, rows, DMA((17 + PIECES,))],
+        6 * 128 * N * N, 6 << 20, limit=64000 << 10,
     )
     take = lax.all_to_all(send, AXES, split_axis=0, concat_axis=0, tiled=True)
     part, mixed, ends = call(
-        part_kernel, parts + [ends], (force, inverse_radii, mode_to_layer), [rows, rates, mixing, *parts, DMA((5,))],
-        1 << 24, 1 << 20, [index], limit=50000 << 10, kept=1,
+        part_kernel, [*parts, ends], (kept,), [rows, DMA((1,))], 1 << 24, 1 << 20, [index], limit=50000 << 10, kept=3
     )
     (give,) = call(
         scan_kernel, [packet], (), [packet, DMA((1,))], 1 << 22, 1 << 18, (), [take, ends], limit=54500 << 10,
     )
     amplitude = lax.all_to_all(give, AXES, split_axis=0, concat_axis=0, tiled=True)
-    (coef,) = call(
-        weight_kernel, [weights], (vorticity, wind_curl, wet_mask, give),
-        [field, plane, ((ROWS, N), i32), weights, DMA((7,))],
-        1 << 24, 5 << 20,
-    )
     return tuple(
         call(
             backward_kernel, [field, field],
-            (coef,),
-            [weights, wave, edge, edge, wave, field, field, DMA((NL + 6,))],
-            6 * 160 * N * N, 10 << 20, [index], [amplitude, part, mixed, table], limit=51500 << 10,
+            (kept,), [field, wave, edge, edge, ((8, NL, N), f32), wave, field, field, DMA((9,))],
+            6 * 160 * N * N, 6 << 20, [index], [amplitude, part, mixed, table, wet_mask, wind_curl], limit=51500 << 10,
         )
     )
 

time: 48.5 us -> 46.5 us (0.959)
  blocking collectives: 0 us -> 15 us
  Pallas kernels: 16 us -> 8.65 us
  waiting for transfers between devices: 13.7 us -> 8.3 us
  starting transfers between devices: 15.3 us -> 11.5 us
    all_to_all x0 -> x1, blocking collectives: none -> 15 us  [body(): lax.all_to_all(give, AXES, split_axis=0, concat_axis=0, tiled=True)]
    pallas_call x5 -> x4, Pallas kernels: 16 us -> 8.65 us  [call(): pl.pallas_call(kernel, out_shape=[jax.ShapeDtypeStruct(s, d) for s, d in...]
    all_to_all x1 -> x0, waiting for transfers between devices: 6.75 us -> none  [body(): lax.all_to_all(give, AXES, split_axis=0, concat_axis=0, tiled=True)]
    all_to_all x1 -> x0, starting transfers between devices: 3.82 us -> none  [body(): lax.all_to_all(give, AXES, split_axis=0, concat_axis=0, tiled=True)]
    all_to_all x1, waiting for transfers between devices: 6.98 us -> 8.3 us  [body(): take = lax.all_to_all(send, AXES, split_axis=0, concat_axis=0, tiled=True)]
  transfers between devices with their start and end apart: 2 -> 1, of which waited for: 2 -> 1; matrix products, arithmetic and copies ran while one was open for 0% -> 0% of each run, Pallas kernels for 14% -> 2%
where the time goes in v4:
time: 46.5 us; the launch traced here: 46.2 us
  blocking collectives  15 us (32%)
  starting transfers between devices  11.5 us (25%)
  Pallas kernels  8.65 us (19%)
  waiting for transfers between devices  8.3 us (18%)
  local copies, waits for them, and re-layouts  2.04 us (4%)
  between operations  0.7 us (2%)
    all_to_all x1, blocking collectives, body(): lax.all_to_all(give, AXES, split_axis=0, concat_axis=0, tiled=True)  15 us
    all_to_all x1, starting transfers between devices, body(): take = lax.all_to_all(send, AXES, split_axis=0, concat_axis=0, tiled=True)  11.5 us
    pallas_call x4, Pallas kernels, call(): pl.pallas_call(kernel, out_shape=[jax.ShapeDtypeStruct(s, d) for s, d in...  8.65 us
    all_to_all x1, waiting for transfers between devices, body(): take = lax.all_to_all(send, AXES, split_axis=0, concat_axis=0, tiled=True)  8.3 us
    unnamed x8, local copies, waits for them, and re-layouts  2.04 us
  transfers between devices with their start and end apart: 1, of which 1 were waited for; matrix products, arithmetic and copies ran while one was open for 0% of the time, Pallas kernels for 2%

profile of v4, /device:TPU:1, one launch (start us, length us, event | category | flops | bytes accessed | tf_op | source)
XLA Modules:
  0.0 46.2 jit_solution(1885404374382750457)
XLA Ops:
  0.6 0.0 copy-start.2
  0.6 0.0 copy-start.3
  0.7 3.6 %shard_map.86 = (f32[128,1,512]{2,1,0:T(1,128)}, f32[112,8,1024]{2,1,0:T(8,128)}) custom-call(f32[16,8,1024]{2,1,0:T(8,128)} %vortex_hbm.1, f32[16,16]{1,0:T(8,128)} %mix_hbm.1, f32[16,16]{1,0:T(8,128)} %back_hbm.1, f32[16]{0:T(128)} %radii_hbm.1, bf16[2,2,512,512]{3,2,1,0:T(8,128)(2,1)} %constant.13.clone.table_hbm.table_ref), custom_call_target="tpu_custom_call" | custom-call | flops 805306368 | bytes 6291456 | tf_op jit(solution)/shard_map/pallas_call | solution.py:346
  4.3 11.5 %all-to-all-start = ((f32[128,1,512]{2,1,0:T(1,128)}), f32[128,1,512]{2,1,0:T(1,128)S(1)}, u32[]{:S(2)}, u32[]{:S(2)}) async-start(f32[128,1,512]{2,1,0:T(1,128)} %get-tuple-element.7), calls=%async_computation | async-start | bytes 524288 | tf_op jit(solution)/shard_map/all_to_all | solution.py:379
  15.8 0.0 copy-start
  15.8 2.0 %copy-done = f32[112,8,1024]{2,1,0:T(8,128)S(1)} copy-done((f32[112,8,1024]{2,1,0:T(8,128)S(1)}, f32[112,8,1024]{2,1,0:T(8,128)}, u32[]{:S(2)}) %copy-start) | copy-done | bytes 3670040
  17.8 0.0 copy-start.1
  17.8 1.1 %shard_map.87 = (f32[11,16,1024]{2,1,0:T(8,128)S(1)}, f32[160,160]{1,0:T(8,128)S(1)}, f32[272,128]{1,0:T(8,128)S(1)}) custom-call(s32[1]{0:T(128)} %bitcast.index_ref, f32[112,8,1024]{2,1,0:T(8,128)S(1)} %copy-done), custom_call_target="tpu_custom_call" | custom-call | flops 16777216 | bytes 1048576 | tf_op jit(solution)/shard_map/pallas_call | solution.py:346
  18.9 8.3 %all-to-all-done.take_ref = f32[128,1,512]{2,1,0:T(1,128)S(1)} async-done(((f32[128,1,512]{2,1,0:T(1,128)}), f32[128,1,512]{2,1,0:T(1,128)S(1)}, u32[]{:S(2)}, u32[]{:S(2)}) %all-to-all-start) | async-done | bytes 262176 | tf_op jit(solution)/shard_map/all_to_all | solution.py:379
  27.2 0.5 %shard_map.88 = f32[128,1,512]{2,1,0:T(1,128)S(1)} custom-call(f32[128,1,512]{2,1,0:T(1,128)S(1)} %all-to-all-done.take_ref, f32[272,128]{1,0:T(8,128)S(1)} %get-tuple-element.9.ends_ref), custom_call_target="tpu_custom_call" | custom-call | flops 4194304 | bytes 262144 | tf_op jit(solution)/shard_map/pallas_call | solution.py:346
  27.7 15.0 %all_to_all.10.take_ref = f32[128,1,512]{2,1,0:T(1,128)S(1)} all-to-all(f32[128,1,512]{2,1,0:T(1,128)S(1)} %shard_map.88), channel_id=1, replica_groups=mesh['group'=2,'tile'=64] {'group','tile'}, dimensions={0} | all-to-all | bytes 524288 | tf_op jit(solution)/shard_map/all_to_all | solution.py:386
  42.8 0.0 copy-done.2
  42.8 0.0 copy-done.3
  42.8 0.0 copy-done.1
  42.8 3.4 %shard_map.89 = (f32[16,8,1024]{2,1,0:T(8,128)}, f32[16,8,1024]{2,1,0:T(8,128)}) custom-call(s32[1]{0:T(128)} %bitcast.index_ref, f32[128,1,512]{2,1,0:T(1,128)S(1)} %all_to_all.10.take_ref, f32[11,16,1024]{2,1,0:T(8,128)S(1)} %get-tuple-element.10.part_ref, f32[160,160]{1,0:T(8,128)S(1)} %get-tuple-element.11.mixed_ref, ...), custom_call_target="tpu_custom_call" | custom-call | flops 1006632960 | bytes 6291456 | tf_op jit(solution)/shard_map/pallas_call | solution.py:346
Async XLA Ops:
  0.6 42.2 %copy-start.2 = (s32[8,1024]{1,0:T(8,128)S(1)}, s32[8,1024]{1,0:T(8,128)}, u32[]{:S(2)}) copy-start(s32[8,1024]{1,0:T(8,128)} %wet_ref.1) | copy-start | bytes 98308
  0.6 42.1 %copy-start.3 = (f32[8,1024]{1,0:T(8,128)S(1)}, f32[8,1024]{1,0:T(8,128)}, u32[]{:S(2)}) copy-start(f32[8,1024]{1,0:T(8,128)} %wind_ref.1) | copy-start | bytes 98308
  4.3 23.0 %all-to-all-start = ((f32[128,1,512]{2,1,0:T(1,128)}), f32[128,1,512]{2,1,0:T(1,128)S(1)}, u32[]{:S(2)}, u32[]{:S(2)}) async-start(f32[128,1,512]{2,1,0:T(1,128)} %get-tuple-element.7), calls=%async_computation | async-start | bytes 524288 | tf_op jit(solution)/shard_map/all_to_all | solution.py:379
  15.8 2.0 %copy-start = (f32[112,8,1024]{2,1,0:T(8,128)S(1)}, f32[112,8,1024]{2,1,0:T(8,128)}, u32[]{:S(2)}) copy-start(f32[112,8,1024]{2,1,0:T(8,128)} %get-tuple-element.8.carry_hbm) | copy-start | bytes 11010052
  17.8 25.0 %copy-start.1 = (bf16[2,2,512,512]{3,2,1,0:T(8,128)(2,1)S(1)}, bf16[2,2,512,512]{3,2,1,0:T(8,128)(2,1)}, u32[]{:S(2)}) copy-start(bf16[2,2,512,512]{3,2,1,0:T(8,128)(2,1)} %constant.13.clone.table_hbm.table_ref) | copy-start | bytes 6291460

commit v5 on v4

--- a/solution.py
+++ b/solution.py
@@ -39,6 +39,20 @@
     return np.stack([high, low], 1)
 
 
+def host_waves():
+    found = []
+    for odd in range(2):
+        wave = np.arange(1 + odd, N + 1, 2)
+        angle_a, angle_b = (
+            np.pi * ((place[:, None] * wave[None, :]) % (2 * (N + 1))) / (N + 1)
+            for place in (32 * np.arange(16), np.arange(1, 33))
+        )
+        scale = math.sqrt(2.0 / (N + 1))
+        rows = [np.sin(angle_a), np.cos(angle_a), scale * np.sin(angle_b), scale * np.cos(angle_b)]
+        found.append(np.concatenate(rows, 0).reshape(3, 32, HALF))
+    return np.stack(found).astype(np.float32)
+
+
 def iota(shape, dim):
     return lax.broadcasted_iota(jnp.int32, shape, dim)
 
@@ -113,16 +127,15 @@
 
 
 def forward_kernel(
-    vortex_hbm, mix_hbm, back_hbm, radii_hbm, table_hbm,
+    vortex_hbm, mix_hbm, back_hbm, radii_hbm, wave_hbm,
     send_hbm, carry_hbm,
-    vortex_ref, mix_ref, back_ref, radii_ref, table_ref, send_ref, force_ref, sems,
+    vortex_ref, mix_ref, back_ref, radii_ref, wave_ref, table_ref, send_ref, force_ref, sems,
 ):
     copies = fetch([(mix_hbm, mix_ref), (radii_hbm, radii_ref)], sems)
     layers = [pl.ds(i, 4) for i in range(0, NL, 4)]
     loads = fetch([(vortex_hbm.at[some], vortex_ref.at[some]) for some in layers], sems, 2)
     copies += fetch([(back_hbm, back_ref)], sems, 6)
-    places = [(odd, low, pl.ds(i, STEP)) for odd in range(2) for low in range(2) for i in range(0, HALF, STEP)]
-    waves = fetch([(table_hbm.at[place], table_ref.at[place]) for place in places], sems, 7)
+    waves = fetch([(wave_hbm.at[i], wave_ref.at[i]) for i in range(2)], sems, 7)
     rows = NL * ROWS
     spread = (iota((NL, rows), 1) // ROWS == iota((NL, rows), 0)).astype(jnp.float32)
     wait(copies[:2])
@@ -131,21 +144,28 @@
     wide = dot(mix_ref[...], spread, HIGHEST)
     mix = jnp.concatenate([wide] * ROWS, 0)
     mix = jnp.where(iota((rows, rows), 0) // NL == iota((rows, rows), 1) % ROWS, mix, 0.0)
-    wait(loads)
-    written = []
+    wait(loads + waves)
+    written = fetch([(vortex_ref, carry_hbm.at[pl.ds(2 * TALL, NL)])], sems, 16 + PIECES)
     high, low = halves(mix)
     mix = jnp.concatenate([jnp.concatenate([high, high], 1), jnp.concatenate([low, jnp.zeros_like(low)], 1)], 0)
     modal = dot(mix, jnp.concatenate(halves(vortex_ref[...].reshape(rows, N)), 0))
     modal = modal[:rows] + modal[rows:]
+    wait(copies[2:])
+    force_ref[2 * ROWS + 2 :, :, :NL] = back_ref[...].reshape(2, ROWS, NL)
+    rest = pl.ds(2 * ROWS, 4)
+    written += fetch([(force_ref.at[rest], carry_hbm.at[rest])], sems, 15 + PIECES)
     mirror = mirrored(modal[:, HALF:])
     folded = [halves(modal[:, :HALF] + mirror), halves(modal[:, :HALF] - mirror)]
     for n in range(PIECES):
         cols = slice(n * STEP, (n + 1) * STEP)
         odd, start = divmod(n * STEP, HALF)
         if start == 0:
-            wait(waves[4 * odd : 4 * odd + 4])
-            if odd:
-                written += fetch([(vortex_ref, carry_hbm.at[pl.ds(2 * TALL, NL)])], sems, 16 + PIECES)
+            for a in range(16):
+                block = wave_ref[odd, 0, a : a + 1] * wave_ref[odd, 2]
+                block += wave_ref[odd, 0, 16 + a : 17 + a] * wave_ref[odd, 1]
+                high, low = halves(block)
+                table_ref[odd, 0, 32 * a : 32 * a + 32] = high
+                table_ref[odd, 1, 32 * a : 32 * a + 32] = low
         some = slice(start, start + STEP)
         spectrum = split_dot(folded[odd], (table_ref[odd, 0, :, some], table_ref[odd, 1, :, some]))
         right = jnp.zeros((NL, STEP), jnp.float32)
@@ -167,9 +187,8 @@
             send_ref[dest * NL : (dest + 1) * NL, 0, 3 * LANES :] = vortex_ref[:, 0, part]
         dests = pl.ds(n * (STEP // LANES) * NL, STEP // LANES * NL)
         written += fetch([(send_ref.at[dests], send_hbm.at[dests])], sems, 15 + n)
-    wait(copies[2:])
-    force_ref[2 * ROWS + 2 :, :, :NL] = back_ref[...].reshape(2, ROWS, NL)
-    written += fetch([(force_ref, carry_hbm.at[pl.ds(0, 2 * TALL)])], sems, 15 + PIECES)
+        some = pl.ds(0, 2 * ROWS), slice(None), pl.ds(n * STEP, STEP)
+        written += fetch([(force_ref.at[some], carry_hbm.at[some])], sems, 17 + PIECES + n)
     wait(written)
 
 
@@ -251,9 +270,13 @@
 
 def roll_lanes(value, step):
     width = value.shape[1]
-    lane = iota(value.shape, 1)
     rolled = pltpu.roll(value, step % width, 1)
-    return jnp.where(lane == (0 if step > 0 else width - 1), 0.0, rolled)
+    lane = iota((value.shape[0], LANES), 1)
+    if step > 0:
+        edge = jnp.where(lane == 0, 0.0, rolled[:, :LANES])
+        return jnp.concatenate([edge, rolled[:, LANES:]], 1)
+    edge = jnp.where(lane == LANES - 1, 0.0, rolled[:, -LANES:])
+    return jnp.concatenate([rolled[:, :-LANES], edge], 1)
 
 
 def roll_sub(value, edge, step):
@@ -304,34 +327,31 @@
     wait(loads)
     keep = time_step * wet_ref[...].astype(jnp.float32)
     twelfth = keep * (1.0 / 12.0)
-    edges = [inside_low * wave_ref[body : body + NL], inside_high * wave_ref[body + NL :], south_ref[...], north_ref[...]]
-    for i, edge in enumerate(edges):
-        edge_ref[2 * i] = edge
-        edge_ref[2 * i + 1] = difference(edge)
+    streams = inside_low * wave_ref[body : body + NL], inside_high * wave_ref[body + NL :]
+    for side, (stream, old) in enumerate(zip(streams, (south_ref[...], north_ref[...]))):
+        edge_ref[3 * side] = stream
+        edge_ref[3 * side + 1] = old
+        edge_ref[3 * side + 2] = difference(old) * stream - old * difference(stream)
     for layer in range(NL):
-        below, across_below, above, across_above, old_below, old_across_below, old_above, old_across_above = (
-            edge_ref[i, layer : layer + 1] for i in range(8)
-        )
+        rows = [edge_ref[i, layer : layer + 1] for i in range(6)]
+
+        def rise(value, i):
+            return roll_sub(value, rows[3 + i], -1) - roll_sub(value, rows[i], 1)
+
+        mid = stream_ref[layer]
         old = given_ref[layer]
-        old_across = difference(old)
-        old_north = roll_sub(old, old_above, -1)
-        old_south = roll_sub(old, old_below, 1)
-        mid = stream_ref[layer]
         east, west = roll_lanes(mid, -1), roll_lanes(mid, 1)
-        across = east - west
-        north = roll_sub(mid, above, -1)
-        south = roll_sub(mid, below, 1)
-        along = north - south
-        mixture = (old_north - old_south + 12.0 * 0.5 * beta_plane) * mid - old * along
-        total = old_south * (across + roll_sub(across, across_below, 1))
-        total -= old_north * (across + roll_sub(across, across_above, -1))
-        total += old_across * along - difference(mixture)
-        total += roll_sub(old_across, old_across_above, -1) * north - roll_sub(old_across, old_across_below, 1) * south
+        across, along = east - west, rise(mid, 0)
+        old_across, old_along = difference(old), rise(old, 1)
+        total = old_across * along - old_along * across
+        total += rise(old_across * mid - old * across, 2)
+        total -= difference((old_along + 12.0 * 0.5 * beta_plane) * mid - old * along)
         total = old + twelfth * total
         if layer == 0:
             total += keep * wind_ref[...]
         if layer == NL - 1:
-            total -= (bottom_drag * keep) * (north + south + east + west - 4.0 * mid)
+            both = roll_sub(mid, rows[3], -1) + roll_sub(mid, rows[0], 1)
+            total -= (bottom_drag * keep) * (both + east + west - 4.0 * mid)
         vortex_ref[layer] = total
         if layer % 4 == 3:
             some = slice(layer - 3, layer + 1)
@@ -372,8 +392,8 @@
     outs = [packet, carry]
     table = jnp.asarray(host_table())
     send, kept = call(
-        forward_kernel, outs, (vorticity, layer_to_mode, mode_to_layer, inverse_radii, table),
-        [field, mixing, mixing, rates, sines, packet, rows, DMA((17 + PIECES,))],
+        forward_kernel, outs, (vorticity, layer_to_mode, mode_to_layer, inverse_radii, jnp.asarray(host_waves())),
+        [field, mixing, mixing, rates, ((2, 3, 32, HALF), f32), sines, packet, rows, DMA((17 + 2 * PIECES,))],
         6 * 128 * N * N, 6 << 20, limit=64000 << 10,
     )
     take = lax.all_to_all(send, AXES, split_axis=0, concat_axis=0, tiled=True)
@@ -387,7 +407,7 @@
     return tuple(
         call(
             backward_kernel, [field, field],
-            (kept,), [field, wave, edge, edge, ((8, NL, N), f32), wave, field, field, DMA((9,))],
+            (kept,), [field, wave, edge, edge, ((6, NL, N), f32), wave, field, field, DMA((9,))],
             6 * 160 * N * N, 6 << 20, [index], [amplitude, part, mixed, table, wet_mask, wind_curl], limit=51500 << 10,
         )
     )

time: 46.5 us -> 46.3 us (level)
  no operation moved by 1% of the time
where the time goes in v5:
time: 46.3 us; the launch traced here: 46 us
  blocking collectives  15 us (32%)
  starting transfers between devices  11.5 us (25%)
  Pallas kernels  8.45 us (18%)
  waiting for transfers between devices  8.3 us (18%)
  local copies, waits for them, and re-layouts  2.04 us (4%)
  between operations  0.7 us (2%)
    all_to_all x1, blocking collectives, body(): lax.all_to_all(give, AXES, split_axis=0, concat_axis=0, tiled=True)  15 us
    all_to_all x1, starting transfers between devices, body(): take = lax.all_to_all(send, AXES, split_axis=0, concat_axis=0, tiled=True)  11.5 us
    pallas_call x4, Pallas kernels, call(): pl.pallas_call(kernel, out_shape=[jax.ShapeDtypeStruct(s, d) for s, d in...  8.45 us
    all_to_all x1, waiting for transfers between devices, body(): take = lax.all_to_all(send, AXES, split_axis=0, concat_axis=0, tiled=True)  8.3 us
    unnamed x8, local copies, waits for them, and re-layouts  2.04 us
  transfers between devices with their start and end apart: 1, of which 1 were waited for; matrix products, arithmetic and copies ran while one was open for 0% of the time, Pallas kernels for 2%

profile of v5, /device:TPU:1, one launch (start us, length us, event | category | flops | bytes accessed | tf_op | source)
XLA Modules:
  0.0 46.0 jit_solution(17869540890570221853)
XLA Ops:
  0.6 0.0 copy-start.2
  0.6 0.0 copy-start.3
  0.7 3.6 %shard_map.95 = (f32[128,1,512]{2,1,0:T(1,128)}, f32[112,8,1024]{2,1,0:T(8,128)}) custom-call(f32[16,8,1024]{2,1,0:T(8,128)} %vortex_hbm.1, f32[16,16]{1,0:T(8,128)} %mix_hbm.1, f32[16,16]{1,0:T(8,128)} %back_hbm.1, f32[16]{0:T(128)} %radii_hbm.1, f32[2,3,32,512]{3,2,1,0:T(8,128)} %constant.16.clone.wave_hbm), custom_call_target="tpu_custom_call" | custom-call | flops 805306368 | bytes 6291456 | tf_op jit(solution)/shard_map/pallas_call | solution.py:366
  4.2 11.5 %all-to-all-start = ((f32[128,1,512]{2,1,0:T(1,128)}), f32[128,1,512]{2,1,0:T(1,128)S(1)}, u32[]{:S(2)}, u32[]{:S(2)}) async-start(f32[128,1,512]{2,1,0:T(1,128)} %get-tuple-element.7), calls=%async_computation | async-start | bytes 524288 | tf_op jit(solution)/shard_map/all_to_all | solution.py:399
  15.7 0.0 copy-start
  15.8 2.0 %copy-done = f32[112,8,1024]{2,1,0:T(8,128)S(1)} copy-done((f32[112,8,1024]{2,1,0:T(8,128)S(1)}, f32[112,8,1024]{2,1,0:T(8,128)}, u32[]{:S(2)}) %copy-start) | copy-done | bytes 3670040
  17.8 0.0 copy-start.1
  17.8 1.1 %shard_map.96 = (f32[11,16,1024]{2,1,0:T(8,128)S(1)}, f32[160,160]{1,0:T(8,128)S(1)}, f32[272,128]{1,0:T(8,128)S(1)}) custom-call(s32[1]{0:T(128)} %bitcast.index_ref, f32[112,8,1024]{2,1,0:T(8,128)S(1)} %copy-done), custom_call_target="tpu_custom_call" | custom-call | flops 16777216 | bytes 1048576 | tf_op jit(solution)/shard_map/pallas_call | solution.py:366
  18.9 8.3 %all-to-all-done.take_ref = f32[128,1,512]{2,1,0:T(1,128)S(1)} async-done(((f32[128,1,512]{2,1,0:T(1,128)}), f32[128,1,512]{2,1,0:T(1,128)S(1)}, u32[]{:S(2)}, u32[]{:S(2)}) %all-to-all-start) | async-done | bytes 262176 | tf_op jit(solution)/shard_map/all_to_all | solution.py:399
  27.2 0.5 %shard_map.97 = f32[128,1,512]{2,1,0:T(1,128)S(1)} custom-call(f32[128,1,512]{2,1,0:T(1,128)S(1)} %all-to-all-done.take_ref, f32[272,128]{1,0:T(8,128)S(1)} %get-tuple-element.9.ends_ref), custom_call_target="tpu_custom_call" | custom-call | flops 4194304 | bytes 262144 | tf_op jit(solution)/shard_map/pallas_call | solution.py:366
  27.7 15.0 %all_to_all.10.take_ref = f32[128,1,512]{2,1,0:T(1,128)S(1)} all-to-all(f32[128,1,512]{2,1,0:T(1,128)S(1)} %shard_map.97), channel_id=1, replica_groups=mesh['group'=2,'tile'=64] {'group','tile'}, dimensions={0} | all-to-all | bytes 524288 | tf_op jit(solution)/shard_map/all_to_all | solution.py:406
  42.7 0.0 copy-done.2
  42.7 0.0 copy-done.3
  42.8 0.0 copy-done.1
  42.8 3.3 %shard_map.98 = (f32[16,8,1024]{2,1,0:T(8,128)}, f32[16,8,1024]{2,1,0:T(8,128)}) custom-call(s32[1]{0:T(128)} %bitcast.index_ref, f32[128,1,512]{2,1,0:T(1,128)S(1)} %all_to_all.10.take_ref, f32[11,16,1024]{2,1,0:T(8,128)S(1)} %get-tuple-element.10.part_ref, f32[160,160]{1,0:T(8,128)S(1)} %get-tuple-element.11.mixed_ref, ...), custom_call_target="tpu_custom_call" | custom-call | flops 1006632960 | bytes 6291456 | tf_op jit(solution)/shard_map/pallas_call | solution.py:366
Async XLA Ops:
  0.6 42.1 %copy-start.2 = (s32[8,1024]{1,0:T(8,128)S(1)}, s32[8,1024]{1,0:T(8,128)}, u32[]{:S(2)}) copy-start(s32[8,1024]{1,0:T(8,128)} %wet_ref.1) | copy-start | bytes 98308
  0.6 42.1 %copy-start.3 = (f32[8,1024]{1,0:T(8,128)S(1)}, f32[8,1024]{1,0:T(8,128)}, u32[]{:S(2)}) copy-start(f32[8,1024]{1,0:T(8,128)} %wind_ref.1) | copy-start | bytes 98308
  4.2 23.0 %all-to-all-start = ((f32[128,1,512]{2,1,0:T(1,128)}), f32[128,1,512]{2,1,0:T(1,128)S(1)}, u32[]{:S(2)}, u32[]{:S(2)}) async-start(f32[128,1,512]{2,1,0:T(1,128)} %get-tuple-element.7), calls=%async_computation | async-start | bytes 524288 | tf_op jit(solution)/shard_map/all_to_all | solution.py:399
  15.7 2.0 %copy-start = (f32[112,8,1024]{2,1,0:T(8,128)S(1)}, f32[112,8,1024]{2,1,0:T(8,128)}, u32[]{:S(2)}) copy-start(f32[112,8,1024]{2,1,0:T(8,128)} %get-tuple-element.8.carry_hbm) | copy-start | bytes 11010052
  17.8 25.0 %copy-start.1 = (bf16[2,2,512,512]{3,2,1,0:T(8,128)(2,1)S(1)}, bf16[2,2,512,512]{3,2,1,0:T(8,128)(2,1)}, u32[]{:S(2)}) copy-start(bf16[2,2,512,512]{3,2,1,0:T(8,128)(2,1)} %constant.15.clone.table_ref) | copy-start | bytes 6291460

commit v6 on v5

--- a/solution.py
+++ b/solution.py
@@ -75,12 +75,19 @@
     return both[:count] + both[count:] + dot(left[0], right[1], None, across)
 
 
-def mirrored(value):
+def mirrored(value, third=False):
     flip = (iota((STEP, STEP), 0) + iota((STEP, STEP), 1) == STEP - 1).astype(jnp.bfloat16)
     count, width = value.shape
-    parts = jnp.concatenate(halves(value), 0)
-    blocks = [dot(parts[:, i : i + STEP], flip) for i in range(0, width, STEP)]
-    return jnp.concatenate([block[:count] + block[count:] for block in reversed(blocks)], 1)
+    parts = list(halves(value))
+    if third:
+        rest = value - parts[0].astype(jnp.float32) - parts[1].astype(jnp.float32)
+        parts.append(rest.astype(jnp.bfloat16))
+    stack = jnp.concatenate(parts, 0)
+    blocks = []
+    for i in reversed(range(0, width, STEP)):
+        block = dot(stack[:, i : i + STEP], flip)
+        blocks.append(sum(block[j * count : (j + 1) * count] for j in reversed(range(len(parts)))))
+    return jnp.concatenate(blocks, 1)
 
 
 def fetch(pairs, sems, first=0):
@@ -132,10 +139,19 @@
     vortex_ref, mix_ref, back_ref, radii_ref, wave_ref, table_ref, send_ref, force_ref, sems,
 ):
     copies = fetch([(mix_hbm, mix_ref), (radii_hbm, radii_ref)], sems)
+    waves = fetch([(wave_hbm.at[i], wave_ref.at[i]) for i in range(2)], sems, 7)
     layers = [pl.ds(i, 4) for i in range(0, NL, 4)]
     loads = fetch([(vortex_hbm.at[some], vortex_ref.at[some]) for some in layers], sems, 2)
     copies += fetch([(back_hbm, back_ref)], sems, 6)
-    waves = fetch([(wave_hbm.at[i], wave_ref.at[i]) for i in range(2)], sems, 7)
+
+    def build(odd):
+        for a in range(16):
+            block = wave_ref[odd, 0, a : a + 1] * wave_ref[odd, 2]
+            block += wave_ref[odd, 0, 16 + a : 17 + a] * wave_ref[odd, 1]
+            high, low = halves(block)
+            table_ref[odd, 0, 32 * a : 32 * a + 32] = high
+            table_ref[odd, 1, 32 * a : 32 * a + 32] = low
+
     rows = NL * ROWS
     spread = (iota((NL, rows), 1) // ROWS == iota((NL, rows), 0)).astype(jnp.float32)
     wait(copies[:2])
@@ -144,7 +160,9 @@
     wide = dot(mix_ref[...], spread, HIGHEST)
     mix = jnp.concatenate([wide] * ROWS, 0)
     mix = jnp.where(iota((rows, rows), 0) // NL == iota((rows, rows), 1) % ROWS, mix, 0.0)
-    wait(loads + waves)
+    waves[0].wait()
+    build(0)
+    wait(loads + waves[1:])
     written = fetch([(vortex_ref, carry_hbm.at[pl.ds(2 * TALL, NL)])], sems, 16 + PIECES)
     high, low = halves(mix)
     mix = jnp.concatenate([jnp.concatenate([high, high], 1), jnp.concatenate([low, jnp.zeros_like(low)], 1)], 0)
@@ -159,13 +177,8 @@
     for n in range(PIECES):
         cols = slice(n * STEP, (n + 1) * STEP)
         odd, start = divmod(n * STEP, HALF)
-        if start == 0:
-            for a in range(16):
-                block = wave_ref[odd, 0, a : a + 1] * wave_ref[odd, 2]
-                block += wave_ref[odd, 0, 16 + a : 17 + a] * wave_ref[odd, 1]
-                high, low = halves(block)
-                table_ref[odd, 0, 32 * a : 32 * a + 32] = high
-                table_ref[odd, 1, 32 * a : 32 * a + 32] = low
+        if odd and start == 0:
+            build(1)
         some = slice(start, start + STEP)
         spectrum = split_dot(folded[odd], (table_ref[odd, 0, :, some], table_ref[odd, 1, :, some]))
         right = jnp.zeros((NL, STEP), jnp.float32)
@@ -311,13 +324,13 @@
             downs.append(downs[-1] * near)
         for i in range(TALL):
             psi_ref[i * NL : (i + 1) * NL, cols] = part_ref[i, :, cols] + ups[i] + downs[ROWS + 1 - i]
-    split = halves(split_dot(halves(mixed_ref[...]), halves(psi_ref[...])))
+    split = halves(dot(mixed_ref[...], psi_ref[...], HIGHEST))
     sums = []
     for odd in range(2):
         some = tuple(part[:, odd * HALF : (odd + 1) * HALF] for part in split)
         sums.append(split_dot(some, (table_ref[odd, 0], table_ref[odd, 1]), 1))
     wave_ref[:, :HALF] = sums[0] + sums[1]
-    wave_ref[:, HALF:] = mirrored(sums[0] - sums[1])
+    wave_ref[:, HALF:] = mirrored(sums[0] - sums[1], True)
     inside_low = jnp.where(index_ref[0] > 0, 1.0, 0.0)
     inside_high = jnp.where(index_ref[0] < BLOCKS - 1, 1.0, 0.0)
     body = NL * ROWS

time: 46.3 us -> 46.5 us (level)
  no operation moved by 1% of the time
where the time goes in v6:
time: 46.5 us; the launch traced here: 46.2 us
  blocking collectives  15 us (32%)
  starting transfers between devices  11.5 us (25%)
  Pallas kernels  8.65 us (19%)
  waiting for transfers between devices  8.3 us (18%)
  local copies, waits for them, and re-layouts  2.04 us (4%)
  between operations  0.7 us (2%)
    all_to_all x1, blocking collectives, body(): lax.all_to_all(give, AXES, split_axis=0, concat_axis=0, tiled=True)  15 us
    all_to_all x1, starting transfers between devices, body(): take = lax.all_to_all(send, AXES, split_axis=0, concat_axis=0, tiled=True)  11.5 us
    pallas_call x4, Pallas kernels, call(): pl.pallas_call(kernel, out_shape=[jax.ShapeDtypeStruct(s, d) for s, d in...  8.65 us
    all_to_all x1, waiting for transfers between devices, body(): take = lax.all_to_all(send, AXES, split_axis=0, concat_axis=0, tiled=True)  8.3 us
    unnamed x8, local copies, waits for them, and re-layouts  2.04 us
  transfers between devices with their start and end apart: 1, of which 1 were waited for; matrix products, arithmetic and copies ran while one was open for 0% of the time, Pallas kernels for 2%

profile of v6, /device:TPU:1, one launch (start us, length us, event | category | flops | bytes accessed | tf_op | source)
XLA Modules:
  0.0 46.2 jit_solution(142645953455523184)
XLA Ops:
  0.6 0.0 copy-start.2
  0.6 0.0 copy-start.3
  0.7 3.5 %shard_map.95 = (f32[128,1,512]{2,1,0:T(1,128)}, f32[112,8,1024]{2,1,0:T(8,128)}) custom-call(f32[16,8,1024]{2,1,0:T(8,128)} %vortex_hbm.1, f32[16,16]{1,0:T(8,128)} %mix_hbm.1, f32[16,16]{1,0:T(8,128)} %back_hbm.1, f32[16]{0:T(128)} %radii_hbm.1, f32[2,3,32,512]{3,2,1,0:T(8,128)} %constant.16.clone.wave_hbm), custom_call_target="tpu_custom_call" | custom-call | flops 805306368 | bytes 6291456 | tf_op jit(solution)/shard_map/pallas_call | solution.py:379
  4.2 11.5 %all-to-all-start = ((f32[128,1,512]{2,1,0:T(1,128)}), f32[128,1,512]{2,1,0:T(1,128)S(1)}, u32[]{:S(2)}, u32[]{:S(2)}) async-start(f32[128,1,512]{2,1,0:T(1,128)} %get-tuple-element.7), calls=%async_computation | async-start | bytes 524288 | tf_op jit(solution)/shard_map/all_to_all | solution.py:412
  15.7 0.0 copy-start
  15.7 2.0 %copy-done = f32[112,8,1024]{2,1,0:T(8,128)S(1)} copy-done((f32[112,8,1024]{2,1,0:T(8,128)S(1)}, f32[112,8,1024]{2,1,0:T(8,128)}, u32[]{:S(2)}) %copy-start) | copy-done | bytes 3670040
  17.7 0.0 copy-start.1
  17.7 1.1 %shard_map.96 = (f32[11,16,1024]{2,1,0:T(8,128)S(1)}, f32[160,160]{1,0:T(8,128)S(1)}, f32[272,128]{1,0:T(8,128)S(1)}) custom-call(s32[1]{0:T(128)} %bitcast.index_ref, f32[112,8,1024]{2,1,0:T(8,128)S(1)} %copy-done), custom_call_target="tpu_custom_call" | custom-call | flops 16777216 | bytes 1048576 | tf_op jit(solution)/shard_map/pallas_call | solution.py:379
  18.8 8.3 %all-to-all-done.take_ref = f32[128,1,512]{2,1,0:T(1,128)S(1)} async-done(((f32[128,1,512]{2,1,0:T(1,128)}), f32[128,1,512]{2,1,0:T(1,128)S(1)}, u32[]{:S(2)}, u32[]{:S(2)}) %all-to-all-start) | async-done | bytes 262176 | tf_op jit(solution)/shard_map/all_to_all | solution.py:412
  27.1 0.5 %shard_map.97 = f32[128,1,512]{2,1,0:T(1,128)S(1)} custom-call(f32[128,1,512]{2,1,0:T(1,128)S(1)} %all-to-all-done.take_ref, f32[272,128]{1,0:T(8,128)S(1)} %get-tuple-element.9.ends_ref), custom_call_target="tpu_custom_call" | custom-call | flops 4194304 | bytes 262144 | tf_op jit(solution)/shard_map/pallas_call | solution.py:379
  27.6 15.0 %all_to_all.10.take_ref = f32[128,1,512]{2,1,0:T(1,128)S(1)} all-to-all(f32[128,1,512]{2,1,0:T(1,128)S(1)} %shard_map.97), channel_id=1, replica_groups=mesh['group'=2,'tile'=64] {'group','tile'}, dimensions={0} | all-to-all | bytes 524288 | tf_op jit(solution)/shard_map/all_to_all | solution.py:419
  42.7 0.0 copy-done.2
  42.7 0.0 copy-done.3
  42.7 0.0 copy-done.1
  42.7 3.5 %shard_map.98 = (f32[16,8,1024]{2,1,0:T(8,128)}, f32[16,8,1024]{2,1,0:T(8,128)}) custom-call(s32[1]{0:T(128)} %bitcast.index_ref, f32[128,1,512]{2,1,0:T(1,128)S(1)} %all_to_all.10.take_ref, f32[11,16,1024]{2,1,0:T(8,128)S(1)} %get-tuple-element.10.part_ref, f32[160,160]{1,0:T(8,128)S(1)} %get-tuple-element.11.mixed_ref, ...), custom_call_target="tpu_custom_call" | custom-call | flops 1006632960 | bytes 6291456 | tf_op jit(solution)/shard_map/pallas_call | solution.py:379
Async XLA Ops:
  0.6 42.0 %copy-start.2 = (s32[8,1024]{1,0:T(8,128)S(1)}, s32[8,1024]{1,0:T(8,128)}, u32[]{:S(2)}) copy-start(s32[8,1024]{1,0:T(8,128)} %wet_ref.1) | copy-start | bytes 98308
  0.6 42.0 %copy-start.3 = (f32[8,1024]{1,0:T(8,128)S(1)}, f32[8,1024]{1,0:T(8,128)}, u32[]{:S(2)}) copy-start(f32[8,1024]{1,0:T(8,128)} %wind_ref.1) | copy-start | bytes 98308
  4.2 23.0 %all-to-all-start = ((f32[128,1,512]{2,1,0:T(1,128)}), f32[128,1,512]{2,1,0:T(1,128)S(1)}, u32[]{:S(2)}, u32[]{:S(2)}) async-start(f32[128,1,512]{2,1,0:T(1,128)} %get-tuple-element.7), calls=%async_computation | async-start | bytes 524288 | tf_op jit(solution)/shard_map/all_to_all | solution.py:412
  15.7 2.0 %copy-start = (f32[112,8,1024]{2,1,0:T(8,128)S(1)}, f32[112,8,1024]{2,1,0:T(8,128)}, u32[]{:S(2)}) copy-start(f32[112,8,1024]{2,1,0:T(8,128)} %get-tuple-element.8.carry_hbm) | copy-start | bytes 11010052
  17.7 25.0 %copy-start.1 = (bf16[2,2,512,512]{3,2,1,0:T(8,128)(2,1)S(1)}, bf16[2,2,512,512]{3,2,1,0:T(8,128)(2,1)}, u32[]{:S(2)}) copy-start(bf16[2,2,512,512]{3,2,1,0:T(8,128)(2,1)} %constant.15.clone.table_ref) | copy-start | bytes 6291460

commit v7 on v6

--- a/solution.py
+++ b/solution.py
@@ -366,9 +366,9 @@
             both = roll_sub(mid, rows[3], -1) + roll_sub(mid, rows[0], 1)
             total -= (bottom_drag * keep) * (both + east + west - 4.0 * mid)
         vortex_ref[layer] = total
-        if layer % 4 == 3:
-            some = slice(layer - 3, layer + 1)
-            written += fetch([(vortex_ref.at[some], vortex_hbm.at[some])], sems, out + 1 + layer // 4)
+        if layer % 2 == 1:
+            some = slice(layer - 1, layer + 1)
+            written += fetch([(vortex_ref.at[some], vortex_hbm.at[some])], sems, out + 1 + layer // 2)
     wait(written)
 
 
@@ -420,7 +420,7 @@
     return tuple(
         call(
             backward_kernel, [field, field],
-            (kept,), [field, wave, edge, edge, ((6, NL, N), f32), wave, field, field, DMA((9,))],
+            (kept,), [field, wave, edge, edge, ((6, NL, N), f32), wave, field, field, DMA((13,))],
             6 * 160 * N * N, 6 << 20, [index], [amplitude, part, mixed, table, wet_mask, wind_curl], limit=51500 << 10,
         )
     )

time: 46.5 us -> 46.5 us (level)
  no operation moved by 1% of the time
where the time goes in v7:
time: 46.5 us; the launch traced here: 46.2 us
  blocking collectives  15 us (32%)
  starting transfers between devices  11.5 us (25%)
  Pallas kernels  8.65 us (19%)
  waiting for transfers between devices  8.3 us (18%)
  local copies, waits for them, and re-layouts  2.04 us (4%)
  between operations  0.7 us (2%)
    all_to_all x1, blocking collectives, body(): lax.all_to_all(give, AXES, split_axis=0, concat_axis=0, tiled=True)  15 us
    all_to_all x1, starting transfers between devices, body(): take = lax.all_to_all(send, AXES, split_axis=0, concat_axis=0, tiled=True)  11.5 us
    pallas_call x4, Pallas kernels, call(): pl.pallas_call(kernel, out_shape=[jax.ShapeDtypeStruct(s, d) for s, d in...  8.65 us
    all_to_all x1, waiting for transfers between devices, body(): take = lax.all_to_all(send, AXES, split_axis=0, concat_axis=0, tiled=True)  8.3 us
    unnamed x8, local copies, waits for them, and re-layouts  2.04 us
  transfers between devices with their start and end apart: 1, of which 1 were waited for; matrix products, arithmetic and copies ran while one was open for 0% of the time, Pallas kernels for 2%

profile of v7, /device:TPU:1, one launch (start us, length us, event | category | flops | bytes accessed | tf_op | source)
XLA Modules:
  0.0 46.2 jit_solution(16734780837256929031)
XLA Ops:
  0.6 0.0 copy-start.2
  0.6 0.0 copy-start.3
  0.7 3.5 %shard_map.95 = (f32[128,1,512]{2,1,0:T(1,128)}, f32[112,8,1024]{2,1,0:T(8,128)}) custom-call(f32[16,8,1024]{2,1,0:T(8,128)} %vortex_hbm.1, f32[16,16]{1,0:T(8,128)} %mix_hbm.1, f32[16,16]{1,0:T(8,128)} %back_hbm.1, f32[16]{0:T(128)} %radii_hbm.1, f32[2,3,32,512]{3,2,1,0:T(8,128)} %constant.16.clone.wave_hbm), custom_call_target="tpu_custom_call" | custom-call | flops 805306368 | bytes 6291456 | tf_op jit(solution)/shard_map/pallas_call | solution.py:379
  4.2 11.5 %all-to-all-start = ((f32[128,1,512]{2,1,0:T(1,128)}), f32[128,1,512]{2,1,0:T(1,128)S(1)}, u32[]{:S(2)}, u32[]{:S(2)}) async-start(f32[128,1,512]{2,1,0:T(1,128)} %get-tuple-element.7), calls=%async_computation | async-start | bytes 524288 | tf_op jit(solution)/shard_map/all_to_all | solution.py:412
  15.7 0.0 copy-start
  15.7 2.0 %copy-done = f32[112,8,1024]{2,1,0:T(8,128)S(1)} copy-done((f32[112,8,1024]{2,1,0:T(8,128)S(1)}, f32[112,8,1024]{2,1,0:T(8,128)}, u32[]{:S(2)}) %copy-start) | copy-done | bytes 3670040
  17.7 0.0 copy-start.1
  17.7 1.1 %shard_map.96 = (f32[11,16,1024]{2,1,0:T(8,128)S(1)}, f32[160,160]{1,0:T(8,128)S(1)}, f32[272,128]{1,0:T(8,128)S(1)}) custom-call(s32[1]{0:T(128)} %bitcast.index_ref, f32[112,8,1024]{2,1,0:T(8,128)S(1)} %copy-done), custom_call_target="tpu_custom_call" | custom-call | flops 16777216 | bytes 1048576 | tf_op jit(solution)/shard_map/pallas_call | solution.py:379
  18.8 8.3 %all-to-all-done.take_ref = f32[128,1,512]{2,1,0:T(1,128)S(1)} async-done(((f32[128,1,512]{2,1,0:T(1,128)}), f32[128,1,512]{2,1,0:T(1,128)S(1)}, u32[]{:S(2)}, u32[]{:S(2)}) %all-to-all-start) | async-done | bytes 262176 | tf_op jit(solution)/shard_map/all_to_all | solution.py:412
  27.1 0.5 %shard_map.97 = f32[128,1,512]{2,1,0:T(1,128)S(1)} custom-call(f32[128,1,512]{2,1,0:T(1,128)S(1)} %all-to-all-done.take_ref, f32[272,128]{1,0:T(8,128)S(1)} %get-tuple-element.9.ends_ref), custom_call_target="tpu_custom_call" | custom-call | flops 4194304 | bytes 262144 | tf_op jit(solution)/shard_map/pallas_call | solution.py:379
  27.6 15.0 %all_to_all.10.take_ref = f32[128,1,512]{2,1,0:T(1,128)S(1)} all-to-all(f32[128,1,512]{2,1,0:T(1,128)S(1)} %shard_map.97), channel_id=1, replica_groups=mesh['group'=2,'tile'=64] {'group','tile'}, dimensions={0} | all-to-all | bytes 524288 | tf_op jit(solution)/shard_map/all_to_all | solution.py:419
  42.7 0.0 copy-done.2
  42.7 0.0 copy-done.3
  42.7 0.0 copy-done.1
  42.7 3.5 %shard_map.98 = (f32[16,8,1024]{2,1,0:T(8,128)}, f32[16,8,1024]{2,1,0:T(8,128)}) custom-call(s32[1]{0:T(128)} %bitcast.index_ref, f32[128,1,512]{2,1,0:T(1,128)S(1)} %all_to_all.10.take_ref, f32[11,16,1024]{2,1,0:T(8,128)S(1)} %get-tuple-element.10.part_ref, f32[160,160]{1,0:T(8,128)S(1)} %get-tuple-element.11.mixed_ref, ...), custom_call_target="tpu_custom_call" | custom-call | flops 1006632960 | bytes 6291456 | tf_op jit(solution)/shard_map/pallas_call | solution.py:379
Async XLA Ops:
  0.6 42.0 %copy-start.2 = (s32[8,1024]{1,0:T(8,128)S(1)}, s32[8,1024]{1,0:T(8,128)}, u32[]{:S(2)}) copy-start(s32[8,1024]{1,0:T(8,128)} %wet_ref.1) | copy-start | bytes 98308
  0.6 42.0 %copy-start.3 = (f32[8,1024]{1,0:T(8,128)S(1)}, f32[8,1024]{1,0:T(8,128)}, u32[]{:S(2)}) copy-start(f32[8,1024]{1,0:T(8,128)} %wind_ref.1) | copy-start | bytes 98308
  4.2 23.0 %all-to-all-start = ((f32[128,1,512]{2,1,0:T(1,128)}), f32[128,1,512]{2,1,0:T(1,128)S(1)}, u32[]{:S(2)}, u32[]{:S(2)}) async-start(f32[128,1,512]{2,1,0:T(1,128)} %get-tuple-element.7), calls=%async_computation | async-start | bytes 524288 | tf_op jit(solution)/shard_map/all_to_all | solution.py:412
  15.7 2.0 %copy-start = (f32[112,8,1024]{2,1,0:T(8,128)S(1)}, f32[112,8,1024]{2,1,0:T(8,128)}, u32[]{:S(2)}) copy-start(f32[112,8,1024]{2,1,0:T(8,128)} %get-tuple-element.8.carry_hbm) | copy-start | bytes 11010052
  17.7 25.0 %copy-start.1 = (bf16[2,2,512,512]{3,2,1,0:T(8,128)(2,1)S(1)}, bf16[2,2,512,512]{3,2,1,0:T(8,128)(2,1)}, u32[]{:S(2)}) copy-start(bf16[2,2,512,512]{3,2,1,0:T(8,128)(2,1)} %constant.15.clone.table_ref) | copy-start | bytes 6291460
